TPU v7x, 32 devices: a whole 2x2x4 slice. The times are simulated.
32 devices in a mesh: dp: 8 (over z, y), mp: 4 (over x, core).
Axes of the slice: x: 2, y: 2, z: 4, core: 2. Of those that a mesh axis runs over, the one named last changes fastest.
Arguments:
- tokens: bfloat16 [8192, 1024], P(('dp', 'mp')), may hold values from -6 to 6
- w_attn: bfloat16 [1024, 4, 1024], P('mp'), may hold values from -4 to 4
- w_ffn: bfloat16 [4096, 2, 1024], P('mp'), may hold values from -4 to 4
- ada_attn: float32 [8, 2, 1024], replicated, may hold values from -2.5 to 2.5
- ada_ffn: float32 [8, 2, 1024], replicated, may hold values from -2.5 to 2.5
- codebook: int32 [8], replicated, may hold values from 0 to 7
- group_sizes: int32 [2], replicated, may hold values from 1 to 6, 8 in all
- partner_pick: int32 [8], replicated, may hold values from 0 to 23
- prompt_start: int32 [8], replicated, may hold values from 0 to 768
- prompt_len: int32 [8], replicated, may hold values from 64 to 256, as said below
- cotangent: bfloat16 [8192, 1024], P(('dp', 'mp')), may hold values from -6 to 6
Outputs:
- output: bfloat16 [8192, 1024], P(('dp', 'mp'))
- grad_tokens: bfloat16 [8192, 1024], P(('dp', 'mp'))
- grad_attn: float32 [1024, 4, 1024], P('mp', None, 'dp')
- grad_ffn: float32 [4096, 2, 1024], P('mp', None, 'dp')
- grad_ada_attn: float32 [8, 2, 1024], P(None, None, ('dp', 'mp'))
- grad_ada_ffn: float32 [8, 2, 1024], P(None, None, ('dp', 'mp'))
Inputs may be any that keep to these rules, and one draw needn't show every extreme that they name: `group_sizes`: the sizes sum to 8. `prompt_len`: some row offers exactly 256 frames.
All inputs are finite; a program needn't handle non-finite values.
Results may differ from a plain program's by a relative error of at most 0.019.
Values may be sent and summed in bfloat16 or wider, within the bound.
A program may use at most 128 MiB of HBM per device.

v0:
```python
import jax
import jax.numpy as jnp
from jax import lax
from jax.sharding import PartitionSpec as P

HD = 64
LEN = 1024
PMAX = 256


epsilon = 1e-05
highest = lax.Precision.HIGHEST


def partner_rows(group_sizes, partner_pick):
    group_end = jnp.cumsum(group_sizes)
    begins = group_end - group_sizes
    row_ids = jnp.arange(partner_pick.shape[0], dtype=jnp.int32)
    owner_group = jnp.sum((group_end[None, :] <= row_ids[:, None]).astype(jnp.int32), axis=1)
    member = (
        owner_group[:, None] == jnp.arange(group_sizes.shape[0], dtype=jnp.int32)[None, :]
    ).astype(jnp.int32)
    first_row = jnp.sum(member * begins[None, :], axis=1)
    group_len = jnp.sum(member * group_sizes[None, :], axis=1)
    span_size = jnp.maximum(group_len - 1, 1)
    return first_row + (row_ids - first_row + 1 + partner_pick % span_size) % group_len


def adaptive_norm(inputs, table, code_hot):
    coefficients = jnp.dot(code_hot, table.reshape(table.shape[0], -1), precision=highest)
    coefficients = coefficients.reshape(inputs.shape[0], 2, inputs.shape[1])
    center = inputs - jnp.mean(inputs, axis=-1, keepdims=True)
    spread = jnp.mean(center * center, axis=-1, keepdims=True)
    normed = center * lax.rsqrt(spread + epsilon)
    return (1.0 + coefficients[:, 0, :]) * normed + coefficients[:, 1, :]


def inner_rows(left, right):
    return lax.dot_general(
        left, right, (((0,), (0,)), ((), ())), preferred_element_type=jnp.float32
    )


def inner_cols(left, right):
    return lax.dot_general(
        left, right, (((1,), (1,)), ((), ())), preferred_element_type=jnp.float32
    )


def row_scores(queries, key_rows, far_valid):
    key_mask = jnp.concatenate([jnp.ones((queries.shape[0],), dtype=jnp.bool_), far_valid])
    scores = jnp.einsum(
        "qhd,khd->hqk", queries, key_rows, preferred_element_type=jnp.float32
    ) * HD ** (-0.5)
    return jnp.where(key_mask[None, None, :], scores, -1000000000.0)


def attend(packed):
    queries, own_keys, own_values, far_keys, far_values, far_valid = packed
    key_rows = jnp.concatenate([own_keys, far_keys], axis=0)
    value_rows = jnp.concatenate([own_values, far_values], axis=0)
    scores = row_scores(queries, key_rows, far_valid)
    row_max = jnp.max(scores, axis=-1, keepdims=True)
    log_total = row_max + jnp.log(jnp.sum(jnp.exp(scores - row_max), axis=-1, keepdims=True))
    prob_low = jnp.exp(scores - log_total).astype(jnp.bfloat16)
    mixed = jnp.einsum("hqk,khd->qhd", prob_low, value_rows, preferred_element_type=jnp.float32)
    return (mixed.astype(jnp.bfloat16), log_total)


def attend_back(packed):
    queries, own_keys, own_values, far_keys, far_values, far_valid, log_total, d_mixed = packed
    key_rows = jnp.concatenate([own_keys, far_keys], axis=0)
    value_rows = jnp.concatenate([own_values, far_values], axis=0)
    scores = row_scores(queries, key_rows, far_valid)
    attn_prob = jnp.exp(scores - log_total)
    prob_low = attn_prob.astype(jnp.bfloat16)
    d_values = jnp.einsum("hqk,qhd->khd", prob_low, d_mixed, preferred_element_type=jnp.float32)
    d_prob = jnp.einsum("qhd,khd->hqk", d_mixed, value_rows, preferred_element_type=jnp.float32)
    row_delta = jnp.sum(attn_prob * d_prob, axis=-1, keepdims=True)
    d_scores = (attn_prob * (d_prob - row_delta)).astype(jnp.bfloat16)
    d_queries = jnp.einsum(
        "hqk,khd->qhd", d_scores, key_rows, preferred_element_type=jnp.float32
    ) * HD ** (-0.5)
    d_keys = jnp.einsum(
        "hqk,qhd->khd", d_scores, queries, preferred_element_type=jnp.float32
    ) * HD ** (-0.5)
    own_len = queries.shape[0]
    return (d_queries, d_keys[:own_len], d_values[:own_len], d_keys[own_len:], d_values[own_len:])


def shards(
    tokens,
    w_attn,
    w_ffn,
    ada_attn,
    ada_ffn,
    codebook,
    group_sizes,
    partner_pick,
    prompt_start,
    prompt_len,
    cotangent,
):
    tok_rows, width = tokens.shape
    mp_size = lax.axis_size("mp")
    dp_index = lax.axis_index("dp")
    mp_index = lax.axis_index("mp")
    block_tokens = tok_rows * mp_size
    seq_here = block_tokens // LEN
    head_cols = w_attn.shape[0]
    heads_here = head_cols // HD
    total_rows = codebook.shape[0]
    partner = partner_rows(group_sizes, partner_pick)
    first_row = dp_index * seq_here
    tok_global = (dp_index * mp_size + mp_index) * tok_rows + jnp.arange(tok_rows, dtype=jnp.int32)
    row_pick = (
        (tok_global // LEN)[:, None] == jnp.arange(total_rows, dtype=jnp.int32)[None, :]
    ).astype(jnp.int32)
    token_codes = jnp.sum(row_pick * codebook[None, :], axis=1)
    code_hot = (
        token_codes[:, None] == jnp.arange(ada_attn.shape[0], dtype=jnp.int32)[None, :]
    ).astype(jnp.float32)
    my_partner = lax.dynamic_slice_in_dim(partner, first_row, seq_here)
    my_starts = lax.dynamic_slice_in_dim(prompt_start, first_row, seq_here)
    partner_hot = (my_partner[:, None] == jnp.arange(total_rows, dtype=jnp.int32)[None, :]).astype(
        jnp.int32
    )
    partner_len = jnp.sum(partner_hot * prompt_len[None, :], axis=1)
    far_valid = jnp.arange(PMAX, dtype=jnp.int32)[None, :] < partner_len[:, None]
    inputs = tokens.astype(jnp.float32)
    normed_attn = adaptive_norm(inputs, ada_attn, code_hot).astype(jnp.bfloat16)
    normed_attn_full = lax.all_gather(normed_attn, "mp", axis=0, tiled=True)
    w_qkv = w_attn[:, 0:3, :]
    w_out = w_attn[:, 3, :]
    qkv_low = jnp.einsum(
        "td,jsd->tsj", normed_attn_full, w_qkv, preferred_element_type=jnp.float32
    ).astype(jnp.bfloat16)
    kv_rows = qkv_low[:, 1:3, :].reshape(seq_here, LEN, 2 * head_cols)
    windows = jax.vmap(
        lambda sequence, offset: lax.dynamic_slice_in_dim(sequence, offset, PMAX, 0)
    )(kv_rows, my_starts)
    shard_rows = lax.all_gather(windows, "dp", axis=0, tiled=True)
    row_ids = jnp.arange(shard_rows.shape[0], dtype=jnp.int32)
    picker = (my_partner[:, None] == row_ids[None, :]).astype(jnp.bfloat16)
    prompt_sum = jnp.einsum("kr,rpc->kpc", picker, shard_rows, preferred_element_type=jnp.float32)
    prompt_kv = prompt_sum.astype(jnp.bfloat16)
    queries = qkv_low[:, 0, :].reshape(seq_here, LEN, heads_here, HD)
    own_keys = qkv_low[:, 1, :].reshape(seq_here, LEN, heads_here, HD)
    own_values = qkv_low[:, 2, :].reshape(seq_here, LEN, heads_here, HD)
    far_keys = prompt_kv[:, :, :head_cols].reshape(seq_here, PMAX, heads_here, HD)
    far_values = prompt_kv[:, :, head_cols:].reshape(seq_here, PMAX, heads_here, HD)
    attended, log_total = lax.map(
        attend, (queries, own_keys, own_values, far_keys, far_values, far_valid)
    )
    attn_flat = attended.reshape(block_tokens, head_cols)
    middle = inputs + lax.psum_scatter(
        jnp.dot(attn_flat, w_out, preferred_element_type=jnp.float32).astype(jnp.bfloat16),
        "mp",
        scatter_dimension=0,
        tiled=True,
    ).astype(jnp.float32)
    normed_ffn = adaptive_norm(middle, ada_ffn, code_hot).astype(jnp.bfloat16)
    normed_ffn_full = lax.all_gather(normed_ffn, "mp", axis=0, tiled=True)
    w_up = w_ffn[:, 0, :]
    w_down = w_ffn[:, 1, :]
    up_proj = inner_cols(normed_ffn_full, w_up)
    activated = jax.nn.gelu(up_proj, approximate=False).astype(jnp.bfloat16)
    output = (
        middle
        + lax.psum_scatter(
            jnp.dot(activated, w_down, preferred_element_type=jnp.float32).astype(jnp.bfloat16),
            "mp",
            scatter_dimension=0,
            tiled=True,
        ).astype(jnp.float32)
    ).astype(jnp.bfloat16)
    shard_rows = lax.all_gather(cotangent, "mp", axis=0, tiled=True)
    rows_grad = inner_cols(shard_rows, w_down)
    d_act = rows_grad
    grad_down = inner_rows(activated, shard_rows)
    _, gelu_pull = jax.vjp(lambda values: jax.nn.gelu(values, approximate=False), up_proj)
    d_up = gelu_pull(d_act)[0].astype(jnp.bfloat16)
    d_normed_ffn = lax.psum_scatter(
        jnp.dot(d_up, w_up, preferred_element_type=jnp.float32).astype(jnp.bfloat16),
        "mp",
        scatter_dimension=0,
        tiled=True,
    ).astype(jnp.float32)
    grad_up = inner_rows(d_up, lax.all_gather(normed_ffn, "mp", axis=0, tiled=True))
    _, norm_ffn_pull = jax.vjp(
        lambda values, table: adaptive_norm(values, table, code_hot), middle, ada_ffn
    )
    d_middle_norm, grad_table_ffn = norm_ffn_pull(d_normed_ffn)
    d_middle = cotangent.astype(jnp.float32) + d_middle_norm
    d_branch = d_middle.astype(jnp.bfloat16)
    shard_rows = lax.all_gather(d_branch, "mp", axis=0, tiled=True)
    rows_grad = inner_cols(shard_rows, w_out)
    grad_out_proj = inner_rows(attn_flat, shard_rows)
    d_mixed = rows_grad.astype(jnp.bfloat16).reshape(seq_here, LEN, heads_here, HD)
    d_queries, d_own_keys, d_own_values, d_far_keys, d_far_values = lax.map(
        attend_back,
        (queries, own_keys, own_values, far_keys, far_values, far_valid, log_total, d_mixed),
    )
    prompt_grad = jnp.concatenate(
        [
            d_far_keys.reshape(seq_here, PMAX, head_cols),
            d_far_values.reshape(seq_here, PMAX, head_cols),
        ],
        axis=2,
    )
    row_ids = jnp.arange(lax.axis_size("dp") * seq_here, dtype=jnp.int32)
    picker = (my_partner[:, None] == row_ids[None, :]).astype(jnp.float32)
    returned_kv = lax.psum_scatter(
        jnp.einsum("kr,kpc->rpc", picker, prompt_grad, precision=highest).astype(jnp.bfloat16),
        "dp",
        scatter_dimension=0,
        tiled=True,
    ).astype(jnp.float32)
    d_kv_rows = jnp.concatenate(
        [
            d_own_keys.reshape(seq_here, LEN, head_cols),
            d_own_values.reshape(seq_here, LEN, head_cols),
        ],
        axis=2,
    )
    d_kv_rows = jax.vmap(
        lambda sequence, window, offset: lax.dynamic_update_slice_in_dim(
            sequence, lax.dynamic_slice_in_dim(sequence, offset, PMAX, 0) + window, offset, 0
        )
    )(d_kv_rows, returned_kv, my_starts)
    d_qkv = jnp.stack(
        [
            d_queries.reshape(block_tokens, head_cols),
            d_kv_rows[:, :, :head_cols].reshape(block_tokens, head_cols),
            d_kv_rows[:, :, head_cols:].reshape(block_tokens, head_cols),
        ],
        axis=1,
    ).astype(jnp.bfloat16)
    d_normed_attn = lax.psum_scatter(
        jnp.einsum("tsj,jsd->td", d_qkv, w_qkv, preferred_element_type=jnp.float32).astype(
            jnp.bfloat16
        ),
        "mp",
        scatter_dimension=0,
        tiled=True,
    ).astype(jnp.float32)
    grad_qkv = jnp.einsum(
        "tsj,td->jsd",
        d_qkv,
        lax.all_gather(normed_attn, "mp", axis=0, tiled=True),
        preferred_element_type=jnp.float32,
    )
    _, norm_attn_pull = jax.vjp(
        lambda values, table: adaptive_norm(values, table, code_hot), inputs, ada_attn
    )
    d_inputs_norm, grad_table_attn = norm_attn_pull(d_normed_attn)
    grad_tokens = (d_middle + d_inputs_norm).astype(jnp.bfloat16)
    grad_attn_local = jnp.concatenate([grad_qkv, grad_out_proj[:, None, :]], axis=1)
    grad_ffn_local = jnp.stack([grad_up, grad_down], axis=1)
    grad_attn, grad_ffn = (
        lax.psum_scatter(
            grad_attn_local.astype(jnp.bfloat16), "dp", scatter_dimension=2, tiled=True
        ).astype(jnp.float32),
        lax.psum_scatter(
            grad_ffn_local.astype(jnp.bfloat16), "dp", scatter_dimension=2, tiled=True
        ).astype(jnp.float32),
    )
    grad_ada_attn, grad_ada_ffn = (
        lax.psum_scatter(grad_table_attn, ("dp", "mp"), scatter_dimension=2, tiled=True),
        lax.psum_scatter(grad_table_ffn, ("dp", "mp"), scatter_dimension=2, tiled=True),
    )
    return (output, grad_tokens, grad_attn, grad_ffn, grad_ada_attn, grad_ada_ffn)


def solution(mesh):
    in_specs = (
        P(("dp", "mp"), None),
        P("mp", None, None),
        P("mp", None, None),
        P(),
        P(),
        P(),
        P(),
        P(),
        P(),
        P(),
        P(("dp", "mp"), None),
    )
    out_specs = (
        P(("dp", "mp"), None),
        P(("dp", "mp"), None),
        P("mp", None, "dp"),
        P("mp", None, "dp"),
        P(None, None, ("dp", "mp")),
        P(None, None, ("dp", "mp")),
    )
    return jax.shard_map(shards, mesh=mesh, in_specs=in_specs, out_specs=out_specs, check_vma=False)
```

profile of v0, /device:TPU:0, one launch (start us, length us, event | category | flops | bytes accessed | tf_op | source)
XLA Modules:
  0.0 899.0 jit_solution(11984073841746806581)
XLA Ops:
  18.6 22.8 %all-gather.6.cloned.1.call-done = bf16[1024,1024]{1,0:T(8,128)(2,1)} async-done(((bf16[256,1024]{1,0:T(8,128)(2,1)}), bf16[1024,1024]{1,0:T(8,128)(2,1)}) %all-gather.6.cloned.1.call-update) | async-done | bytes 2097168 | tf_op jit(solution)/shard_map/all_gather | solution.py:132
  41.4 4.3 fusion.38
  47.1 3.7 slice.106
  54.3 42.1 %all-gather.8.cloned.1.call-done = bf16[8,256,512]{2,1,0:T(8,128)(2,1)} async-done(((bf16[1,256,512]{2,1,0:T(8,128)(2,1)}), bf16[8,256,512]{2,1,0:T(8,128)(2,1)}) %all-gather.8.cloned.1.call-update) | async-done | bytes 2097168 | tf_op jit(solution)/shard_map/all_gather | solution.py:142
  104.1 3.8 exponential_reduce_fusion
  111.1 8.9 fusion.41
  124.0 28.9 %reduce-scatter.16.cloned.1.call-done = bf16[256,1024]{1,0:T(8,128)(2,1)} async-done(((bf16[1024,1024]{1,0:T(8,128)(2,1)}), bf16[256,1024]{1,0:T(8,128)(2,1)}) %reduce-scatter.16.cloned.1.call-update) | async-done | bytes 524304 | tf_op jit(solution)/shard_map/reduce_scatter | solution.py:156
  158.6 10.0 %fusion.101 = (bf16[1024,1,1024]{2,1,0:T(2,128)(2,1)}, bf16[1024,1,1024]{2,1,0:T(2,128)(2,1)}) fusion(bf16[1024,2,1024]{2,1,0:T(2,128)(2,1)} %param.15), kind=kLoop, calls=%fused_computation.179 | loop fusion | bytes 8388608 | tf_op jit(solution)/shard_map/slice | solution.py:165
  168.6 11.9 %all-gather.10.cloned.1.call-done = bf16[1024,1024]{1,0:T(8,128)(2,1)} async-done(((bf16[256,1024]{1,0:T(8,128)(2,1)}), bf16[1024,1024]{1,0:T(8,128)(2,1)}) %all-gather.10.cloned.1.call-update) | async-done | bytes 2097168 | tf_op jit(solution)/shard_map/all_gather | solution.py:163
  180.5 16.2 %multiply_convert_fusion.2 = (bf16[1024,1024]{1,0:T(8,128)(2,1)}, f32[1024,1024]{1,0:T(8,128)}, f32[1024,1024]{1,0:T(8,128)}) fusion(bf16[1024,1024]{1,0:T(8,128)(2,1)} %all-gather.10.cloned.1.call-done, bf16[1024,1,1024]{2,1,0:T(2,128)(2,1)} %get-tuple-element.142), kind=kOutput, calls=%fused_computation.12 | convolution fusion | flops 2215641088 | bytes 14680064 | tf_op jit(solution)/shard_map/dot_general | solution.py:45
  196.7 7.9 all-gather.12.cloned.1.call-done
  204.6 8.9 add_convert_fusion
  218.6 6.6 convolution_convert_fusion.1
  225.4 24.8 %reduce-scatter.20.cloned.1.call-done = bf16[256,1024]{1,0:T(8,128)(2,1)} async-done(((bf16[1024,1024]{1,0:T(8,128)(2,1)}), bf16[256,1024]{1,0:T(8,128)(2,1)}) %reduce-scatter.20.cloned.1.call-update) | async-done | bytes 524304 | tf_op jit(solution)/shard_map/reduce_scatter | solution.py:183
  251.6 32.5 %reduce-scatter.18.cloned.1.call-done = bf16[256,1024]{1,0:T(8,128)(2,1)} async-done(((bf16[1024,1024]{1,0:T(8,128)(2,1)}), bf16[256,1024]{1,0:T(8,128)(2,1)}) %reduce-scatter.18.cloned.1.call-update) | async-done | bytes 524304 | tf_op jit(solution)/shard_map/reduce_scatter | solution.py:170
  289.9 22.0 %all-gather.14.cloned.1.call-done = bf16[1024,1024]{1,0:T(8,128)(2,1)} async-done(((bf16[256,1024]{1,0:T(8,128)(2,1)}), bf16[1024,1024]{1,0:T(8,128)(2,1)}) %all-gather.14.cloned.1.call-update) | async-done | bytes 2097168 | tf_op jit(solution)/shard_map/all_gather | solution.py:196
  314.6 9.0 fusion.11
  323.5 13.7 %multiply_reduce_fusion = (f32[4,1024]{1,0:T(4,128)S(1)}, f32[4,1024,1280]{2,1,0:T(8,128)}) fusion(f32[4,1024,1280]{2,1,0:T(8,128)} %copy-done, f32[4,1024]{1,0:T(4,128)S(1)} %log_add_fusion, bf16[1024,4,64]{0,2,1:T(8,128)(2,1)S(1)} %bitcast.209, bf16[256,4,64]{0,2,1:T(8,128)(2,1)S(1)} %bitcast.218, bf16[1024,4,64]{0,2,1:T(8,128)(2,1)S(1)} %bitcast.204), kind=kOutput, calls=%fused_computation.1 | convolution fusion | flops 688123904 | bytes 43155456 | tf_op jit(solution)/shard_map/while/body/eval_jaxpr/qhd,khd->hqk/dot_general | solution.py:78
  337.2 14.2 %multiply_convert_fusion = bf16[4,1024,1280]{2,1,0:T(8,128)(2,1)S(1)} fusion(f32[4,1024,1280]{2,1,0:T(8,128)} %get-tuple-element.159, f32[4,1024,1280]{2,1,0:T(8,128)} %copy-done, f32[4,1024]{1,0:T(4,128)S(1)} %get-tuple-element.158, f32[4,1024]{1,0:T(4,128)S(1)} %log_add_fusion), kind=kLoop, calls=%fused_computation | loop fusion | flops 20971520 | bytes 52461568 | tf_op jit(solution)/shard_map/while/body/eval_jaxpr/convert_element_type | solution.py:80
  358.8 6.1 convert_bitcast_fusion
  364.9 3.8 convert_bitcast_fusion.1
  375.7 4.7 pad_maximum_fusion
  380.4 11.4 %copy.83 = bf16[1024,2,1024]{0,1,2:T(2,128)(2,1)} copy(bf16[1024,2,1024]{2,0,1:T(8,128)(2,1)} %pad_maximum_fusion) | data formatting | bytes 8388608
  391.8 5.7 copy.98
  403.4 7.3 fusion.44
  413.5 13.2 %reduce-scatter.22.cloned.1.call-done = bf16[1,256,512]{2,1,0:T(8,128)(2,1)} async-done(((bf16[8,256,512]{2,1,0:T(8,128)(2,1)}), bf16[1,256,512]{2,1,0:T(8,128)(2,1)}) %reduce-scatter.22.cloned.1.call-update) | async-done | bytes 262160 | tf_op jit(solution)/shard_map/reduce_scatter | solution.py:213
  433.5 4.9 bitcast_convert_fusion
  446.4 116.0 %reduce-scatter.32.cloned.1.call-done = f32[32,16]{1,0:T(8,128)} async-done(((f32[1024,16]{1,0:T(8,128)}), f32[32,16]{1,0:T(8,128)}) %reduce-scatter.32.cloned.1.call-update) | async-done | bytes 2064
  563.9 86.0 %reduce-scatter.28.cloned.1.call-done = bf16[128,2048]{1,0:T(8,128)(2,1)} async-done(((bf16[1024,2048]{1,0:T(8,128)(2,1)}), bf16[128,2048]{1,0:T(8,128)(2,1)}) %reduce-scatter.28.cloned.1.call-update) | async-done | bytes 524304
  655.0 28.7 %reduce-scatter.24.cloned.1.call-done = bf16[256,1024]{1,0:T(8,128)(2,1)} async-done(((bf16[1024,1024]{1,0:T(8,128)(2,1)}), bf16[256,1024]{1,0:T(8,128)(2,1)}) %reduce-scatter.24.cloned.1.call-update) | async-done | bytes 524304 | tf_op jit(solution)/shard_map/reduce_scatter | solution.py:239
  701.0 54.6 %reduce-scatter.26.cloned.1.call-done = bf16[256,4,128]{0,2,1:T(8,128)(2,1)} async-done(((bf16[256,4,1024]{0,2,1:T(8,128)(2,1)}), bf16[256,4,128]{0,2,1:T(8,128)(2,1)}) %reduce-scatter.26.cloned.1.call-update) | async-done | bytes 262160 | tf_op jit(solution)/shard_map/reduce_scatter | solution.py:261
  757.5 133.2 %reduce-scatter.30.cloned.1.call-done = f32[32,16]{1,0:T(8,128)} async-done(((f32[1024,16]{1,0:T(8,128)}), f32[32,16]{1,0:T(8,128)}) %reduce-scatter.30.cloned.1.call-update) | async-done | bytes 2064
  (205 shorter events, 114.4 us)
Async XLA Ops:
  7.2 34.3 %all-gather.6.cloned.1.call-start = ((), (), s32[]{:S(2)}) async-start(), calls=%async_computation.9 | async-start | bytes 2621440 | tf_op jit(solution)/shard_map/all_gather | solution.py:132
  8.4 37.3 %copy-start.28 = (f32[256]{0:T(256)}, f32[256]{0:T(256)S(1)}, u32[]{:S(2)}) copy-start(f32[256]{0:T(256)S(1)} %broadcast_multiply_fusion.1) | copy-start | bytes 3076
  9.8 35.9 %copy-start.32 = (f32[256]{0:T(256)}, f32[256]{0:T(256)S(1)}, u32[]{:S(2)}) copy-start(f32[256]{0:T(256)S(1)} %fusion.51) | copy-start | bytes 3076
  9.8 35.9 %copy-start.30 = (f32[256]{0:T(256)}, f32[256]{0:T(256)S(1)}, u32[]{:S(2)}) copy-start(f32[256]{0:T(256)S(1)} %fusion.85) | copy-start | bytes 3076
  16.0 80.4 %all-gather.8.cloned.1.call-start = ((), (), s32[]{:S(2)}) async-start(), calls=%async_computation.10 | async-start | bytes 2359296 | tf_op jit(solution)/shard_map/all_gather | solution.py:142
  46.9 106.1 %reduce-scatter.16.cloned.1.call-start = ((), (), s32[]{:S(2)}) async-start(), calls=%async_computation.11 | async-start | bytes 2621440 | tf_op jit(solution)/shard_map/reduce_scatter | solution.py:156
  54.2 49.8 %copy-start.8 = (bf16[1024,1,256]{0,2,1:T(8,128)(2,1)}, bf16[1024,1,256]{0,2,1:T(8,128)(2,1)S(1)}, u32[]{:S(2)}) copy-start(bf16[1024,1,256]{0,2,1:T(8,128)(2,1)S(1)} %get-tuple-element.146) | copy-start | bytes 1572868
  54.2 49.8 %copy-start.12 = (bf16[1024,1,256]{0,2,1:T(8,128)(2,1)}, bf16[1024,1,256]{0,2,1:T(8,128)(2,1)S(1)}, u32[]{:S(2)}) copy-start(bf16[1024,1,256]{0,2,1:T(8,128)(2,1)S(1)} %get-tuple-element.145) | copy-start | bytes 1572868
  54.3 56.8 %copy-start.14 = (bf16[1024,1,256]{0,2,1:T(8,128)(2,1)}, bf16[1024,1,256]{0,2,1:T(8,128)(2,1)S(1)}, u32[]{:S(2)}) copy-start(bf16[1024,1,256]{0,2,1:T(8,128)(2,1)S(1)} %get-tuple-element.144) | copy-start | bytes 1572868
  120.0 33.0 %copy-start.2 = (bf16[256,1024]{1,0:T(8,128)(2,1)S(1)}, bf16[256,1024]{1,0:T(8,128)(2,1)}, u32[]{:S(2)}) copy-start(bf16[256,1024]{1,0:T(8,128)(2,1)} %param.13) | copy-start | bytes 1572868
  122.9 57.6 %all-gather.10.cloned.1.call-start = ((), (), s32[]{:S(2)}) async-start(), calls=%async_computation.12 | async-start | bytes 2621440 | tf_op jit(solution)/shard_map/all_gather | solution.py:163
  157.8 46.9 %all-gather.12.cloned.1.call-start = ((), (), s32[]{:S(2)}) async-start(), calls=%async_computation.14 | async-start | bytes 2621440 | tf_op jit(solution)/shard_map/all_gather | solution.py:177
  158.4 91.8 %reduce-scatter.20.cloned.1.call-start = ((), (), s32[]{:S(2)}) async-start(), calls=%async_computation.15 | async-start | bytes 2621440 | tf_op jit(solution)/shard_map/reduce_scatter | solution.py:183
  204.6 10.2 %copy-start.21 = (bf16[1024,1,1024]{2,1,0:T(2,128)(2,1)S(1)}, bf16[1024,1,1024]{2,1,0:T(2,128)(2,1)}, u32[]{:S(2)}) copy-start(bf16[1024,1,1024]{2,1,0:T(2,128)(2,1)} %get-tuple-element.142) | copy-start | bytes 6291460
  218.6 65.6 %reduce-scatter.18.cloned.1.call-start = ((), (), s32[]{:S(2)}) async-start(), calls=%async_computation.13 | async-start | bytes 2621440 | tf_op jit(solution)/shard_map/reduce_scatter | solution.py:170
  218.6 31.5 %copy-start.5 = (bf16[256,1024]{1,0:T(8,128)(2,1)S(1)}, bf16[256,1024]{1,0:T(8,128)(2,1)}, u32[]{:S(2)}) copy-start(bf16[256,1024]{1,0:T(8,128)(2,1)} %reduce-scatter.16.cloned.1.call-done) | copy-start | bytes 1572868
  225.3 86.6 %all-gather.14.cloned.1.call-start = ((), (), s32[]{:S(2)}) async-start(), calls=%async_computation.16 | async-start | bytes 2621440 | tf_op jit(solution)/shard_map/all_gather | solution.py:196
  289.2 137.6 %reduce-scatter.22.cloned.1.call-start = ((), (), s32[]{:S(2)}) async-start(), calls=%async_computation.17 | async-start | bytes 2359296 | tf_op jit(solution)/shard_map/reduce_scatter | solution.py:213
  323.5 13.7 %copy-start.10 = (f32[1280,4,64]{0,2,1:T(8,128)}, f32[1280,4,64]{0,2,1:T(8,128)S(1)}, u32[]{:S(2)}) copy-start(f32[1280,4,64]{0,2,1:T(8,128)S(1)} %fusion.11) | copy-start | bytes 3932164
  337.2 14.2 %copy-start.9 = (bf16[1024,1,256]{0,2,1:T(8,128)(2,1)S(1)}, bf16[1024,1,256]{0,2,1:T(8,128)(2,1)}, u32[]{:S(2)}) copy-start(bf16[1024,1,256]{0,2,1:T(8,128)(2,1)} %copy-done.8) | copy-start | bytes 1572868
  358.8 203.7 %reduce-scatter.32.cloned.1.call-start = ((), (), s32[]{:S(2)}) async-start(), calls=%async_computation.22 | async-start | bytes 540672
  375.7 274.2 %reduce-scatter.28.cloned.1.call-start = ((), (), s32[]{:S(2)}) async-start(), calls=%async_computation.20 | async-start | bytes 4718592
  397.6 286.1 %reduce-scatter.24.cloned.1.call-start = ((), (), s32[]{:S(2)}) async-start(), calls=%async_computation.18 | async-start | bytes 2621440 | tf_op jit(solution)/shard_map/reduce_scatter | solution.py:239
  438.5 317.2 %reduce-scatter.26.cloned.1.call-start = ((), (), s32[]{:S(2)}) async-start(), calls=%async_computation.19 | async-start | bytes 2359296 | tf_op jit(solution)/shard_map/reduce_scatter | solution.py:261
  444.5 239.1 %copy-start.4 = (f32[256,2,1024]{2,0,1:T(8,128)S(1)}, f32[256,2,1024]{2,0,1:T(8,128)}, u32[]{:S(2)}) copy-start(f32[256,2,1024]{2,0,1:T(8,128)} %copy-done.3) | copy-start | bytes 6291460
  444.5 239.1 %copy-start.29 = (f32[256]{0:T(256)S(1)}, f32[256]{0:T(256)}, u32[]{:S(2)}) copy-start(f32[256]{0:T(256)} %copy-done.28) | copy-start | bytes 3076
  446.1 239.0 %copy-start.33 = (f32[256]{0:T(256)S(1)}, f32[256]{0:T(256)}, u32[]{:S(2)}) copy-start(f32[256]{0:T(256)} %copy-done.32) | copy-start | bytes 3076
  446.1 240.1 %copy-start.31 = (f32[256]{0:T(256)S(1)}, f32[256]{0:T(256)}, u32[]{:S(2)}) copy-start(f32[256]{0:T(256)} %copy-done.30) | copy-start | bytes 3076
  446.1 444.6 %reduce-scatter.30.cloned.1.call-start = ((), (), s32[]{:S(2)}) async-start(), calls=%async_computation.21 | async-start | bytes 540672
  690.2 9.7 %copy-start.7 = (f32[256,1024]{1,0:T(8,128)S(1)}, f32[256,1024]{1,0:T(8,128)}, u32[]{:S(2)}) copy-start(f32[256,1024]{1,0:T(8,128)} %copy-done.6) | copy-start | bytes 3145732
  690.2 9.8 %copy-start.18 = (bf16[256,1024]{1,0:T(8,128)(2,1)S(1)}, bf16[256,1024]{1,0:T(8,128)(2,1)}, u32[]{:S(2)}) copy-start(bf16[256,1024]{1,0:T(8,128)(2,1)} %param.23) | copy-start | bytes 1572868
  690.2 9.8 %copy-start.20 = (f32[256,1024]{1,0:T(8,128)S(1)}, f32[256,1024]{1,0:T(8,128)}, u32[]{:S(2)}) copy-start(f32[256,1024]{1,0:T(8,128)} %get-tuple-element.136) | copy-start | bytes 3145732
  (27 other events, 120.7 us)
Sparse Core Ops, SparseCore 0:
  16.1 25.2 all-gather.5
  47.0 49.3 all-gather.7
  123.1 29.8 reduce-scatter.15
  157.9 22.5 all-gather.9
  182.0 22.5 all-gather.11
  218.7 31.4 reduce-scatter.19
  252.7 31.4 reduce-scatter.17
  289.3 22.5 all-gather.13
  358.9 67.8 reduce-scatter.21
  429.5 132.8 reduce-scatter.31
  566.1 83.7 reduce-scatter.27
  652.5 31.1 reduce-scatter.23
  687.2 68.3 reduce-scatter.25
  757.7 132.9 reduce-scatter.29
where the time goes:
time: 904 us; the launch traced here: 899 us
  waiting for transfers between devices  625 us (69%)
  matrix products  121 us (13%)
  local copies, waits for them, and re-layouts  76 us (8%)
  other arithmetic  58.2 us (6%)
  between operations  16.9 us (2%)
    unnamed x17, waiting for transfers between devices  336 us
    reduce_scatter x1, waiting for transfers between devices, shards(): lax.psum_scatter(grad_attn_local.astype(jnp.bfloat16), 'dp', scatter_dime...  54.6 us
    unnamed x101, local copies, waits for them, and re-layouts  45.2 us
    all_gather x1, waiting for transfers between devices, shards(): shard_rows = lax.all_gather(windows, 'dp', axis=0, tiled=True)  42.1 us
    reduce_scatter x1, waiting for transfers between devices, shards(): lax.psum_scatter(jnp.dot(activated, w_down, preferred_element_type=jnp.fl...  32.5 us
    reduce_scatter x1, waiting for transfers between devices, shards(): lax.psum_scatter(jnp.dot(attn_flat, w_out, preferred_element_type=jnp.flo...  28.9 us
    reduce_scatter x1, waiting for transfers between devices, shards(): lax.psum_scatter(jnp.einsum('tsj,jsd->td', d_qkv, w_qkv, preferred_elemen...  28.7 us
    dot_general x3, matrix products, inner_cols(): lax.dot_general(left, right, (((1,), (1,)), ((), ())), preferred_element_...  27.7 us
  transfers between devices with their start and end apart: 14, of which 14 were waited for; matrix products, arithmetic and copies ran while one was open for 16% of the time, Pallas kernels for 0%

commit v1 on v0

--- a/solution.py
+++ b/solution.py
@@ -1,7 +1,15 @@
+import functools
+
 import jax
 import jax.numpy as jnp
 from jax import lax
+from jax.experimental import pallas as pl
+from jax.experimental.pallas import tpu as pltpu
 from jax.sharding import PartitionSpec as P
+
+MESH = pl.DeviceIdType.MESH
+F32 = jnp.float32
+BF16 = jnp.bfloat16
 
 HD = 64
 LEN = 1024
@@ -86,6 +94,203 @@
     ) * HD ** (-0.5)
     own_len = queries.shape[0]
     return (d_queries, d_keys[:own_len], d_values[:own_len], d_keys[own_len:], d_values[own_len:])
+
+
+class Links:
+    def __init__(self, z_size, send_sem, recv_sem):
+        self.dp = lax.axis_index("dp")
+        self.mp = lax.axis_index("mp")
+        self.z_size = z_size
+        self.y = lax.rem(self.dp, 2)
+        self.z = self.dp // 2
+        self.core = lax.rem(self.mp, 2)
+        self.x = self.mp // 2
+        self.sib = (self.dp, self.mp + 1 - 2 * self.core)
+        self.xpeer = (self.dp, self.mp + 2 - 4 * self.x)
+        self.ypeer = (self.dp + 1 - 2 * self.y, self.mp)
+        self.right = (self.dp + 2, self.mp)
+        self.left = (self.dp - 2, self.mp)
+        self.send_sem = send_sem
+        self.recv_sem = recv_sem
+        self.used = 0
+        self.sent = []
+
+    def take(self, count=1):
+        first = self.used
+        self.used += count
+        return first
+
+    def copy(self, src, dst, number, device):
+        return pltpu.make_async_remote_copy(
+            src_ref=src,
+            dst_ref=dst,
+            send_sem=self.send_sem.at[number],
+            recv_sem=self.recv_sem.at[number],
+            device_id=device,
+            device_id_type=MESH,
+        )
+
+    def barrier(self):
+        bar = pltpu.get_barrier_semaphore()
+        for device in (self.sib, self.xpeer, self.ypeer):
+            pl.semaphore_signal(bar, inc=1, device_id=device, device_id_type=MESH)
+
+        @pl.when(self.z > 0)
+        def _():
+            pl.semaphore_signal(bar, inc=1, device_id=self.left, device_id_type=MESH)
+
+        @pl.when(self.z < self.z_size - 1)
+        def _():
+            pl.semaphore_signal(bar, inc=1, device_id=self.right, device_id_type=MESH)
+
+        inner = (self.z > 0).astype(jnp.int32) + (self.z < self.z_size - 1).astype(jnp.int32)
+        pl.semaphore_wait(bar, 3 + inner)
+
+
+class LineReduce:
+    def __init__(self, links, local, from_y, held, from_left, from_right):
+        self.k = links
+        self.local, self.from_y, self.held = local, from_y, held
+        self.from_left, self.from_right = from_left, from_right
+        n = links.z_size
+        self.ny = links.take(n)
+        self.nr = links.take(n)
+        self.nl = links.take(n)
+
+    def y_copy(self, d):
+        k = self.k
+        other = 2 * d + 1 - k.y
+        return k.copy(self.local.at[other], self.from_y.at[d], self.ny + d, k.ypeer)
+
+    def send_y(self, dests=None):
+        for d in dests or range(self.k.z_size):
+            self.y_copy(d).start()
+
+    def z_copy(self, d, rightward):
+        k = self.k
+        if rightward:
+            return k.copy(self.held.at[d], self.from_left.at[d], self.nr + d, k.right)
+        return k.copy(self.held.at[d], self.from_right.at[d], self.nl + d, k.left)
+
+    def add(self, d, what):
+        total = self.held[d].astype(F32) + what[d].astype(F32)
+        self.held[d] = total.astype(self.held.dtype)
+
+    def order(self):
+        n = self.k.z_size
+        return [n - 1, 0] + list(range(1, n - 1))
+
+    def merge_y(self, d):
+        k = self.k
+        self.y_copy(d).wait_recv()
+        total = self.local[2 * d + k.y].astype(F32) + self.from_y[d].astype(F32)
+        self.held[d] = total.astype(self.held.dtype)
+
+    def move(self, d):
+        k = self.k
+
+        @pl.when(k.z < d)
+        def _():
+            @pl.when(k.z > 0)
+            def _():
+                self.z_copy(d, True).wait_recv()
+                self.add(d, self.from_left)
+
+            self.z_copy(d, True).start()
+
+        @pl.when(k.z > d)
+        def _():
+            @pl.when(k.z < k.z_size - 1)
+            def _():
+                self.z_copy(d, False).wait_recv()
+                self.add(d, self.from_right)
+
+            self.z_copy(d, False).start()
+
+    def finish(self, store):
+        k = self.k
+        n = k.z_size
+        for d in range(n):
+
+            @pl.when(k.z == d)
+            def _(d=d):
+                total = self.held[d].astype(F32)
+                if d > 0:
+                    self.z_copy(d, True).wait_recv()
+                    total = total + self.from_left[d].astype(F32)
+                if d < n - 1:
+                    self.z_copy(d, False).wait_recv()
+                    total = total + self.from_right[d].astype(F32)
+                store(total)
+
+    def wait_sends(self):
+        k = self.k
+        for d in range(k.z_size):
+            self.y_copy(d).wait_send()
+
+            @pl.when(k.z < d)
+            def _(d=d):
+                self.z_copy(d, True).wait_send()
+
+            @pl.when(k.z > d)
+            def _(d=d):
+                self.z_copy(d, False).wait_send()
+
+
+def grads_kernel(z_size, heads_rows, ga, gf, ta, out_a, out_f, out_t, *scratch):
+    bufs = scratch[:-2]
+    k = Links(z_size, *scratch[-2:])
+    k.barrier()
+    units = []
+    for local, at in ((gf, 0), (ga, 4), (ta, 8)):
+        units.append(LineReduce(k, local, *bufs[at : at + 4]))
+    for unit in units:
+        unit.send_y(unit.order())
+    for unit in units:
+        for d in unit.order():
+            unit.merge_y(d)
+            unit.move(d)
+    half = gf.shape[1] // 2
+    quarter = ga.shape[1] // 4
+
+    def store_f(total):
+        for s in range(2):
+            out_f[pl.ds(s, half, stride=2), :] = total[s * half : (s + 1) * half]
+
+    def store_a(total):
+        for s in range(4):
+            out_a[pl.ds(s, quarter, stride=4), :] = total[s * quarter : (s + 1) * quarter]
+
+    def store_t(total):
+        out_t[...] = total
+
+    for unit, store in zip(units, (store_f, store_a, store_t)):
+        unit.finish(store)
+    for unit in units:
+        unit.wait_sends()
+
+
+def reduce_grads(ga, gf, ta, dp_size):
+    z_size = dp_size // 2
+    bufs = []
+    for block in (gf, ga, ta):
+        bufs += [pltpu.VMEM((z_size,) + block.shape[1:], block.dtype)] * 4
+    copies = 3 * 3 * z_size
+    return pl.pallas_call(
+        functools.partial(grads_kernel, z_size, 4),
+        out_shape=(
+            jax.ShapeDtypeStruct(ga.shape[1:], F32),
+            jax.ShapeDtypeStruct(gf.shape[1:], F32),
+            jax.ShapeDtypeStruct(ta.shape[1:], F32),
+        ),
+        in_specs=[pl.BlockSpec(memory_space=pltpu.VMEM)] * 3,
+        out_specs=[pl.BlockSpec(memory_space=pltpu.VMEM)] * 3,
+        scratch_shapes=bufs
+        + [pltpu.SemaphoreType.DMA((copies,)), pltpu.SemaphoreType.DMA((copies,))],
+        compiler_params=pltpu.CompilerParams(
+            collective_id=1, has_side_effects=True, vmem_limit_bytes=60 << 20
+        ),
+    )(ga, gf, ta)
 
 
 def shards(
@@ -255,6 +460,31 @@
     )
     d_inputs_norm, grad_table_attn = norm_attn_pull(d_normed_attn)
     grad_tokens = (d_middle + d_inputs_norm).astype(jnp.bfloat16)
+    dp_size = lax.axis_size("dp")
+    lane_block = width // dp_size
+    if lane_block == 128 and seq_here == 1 and dp_size % 2 == 0 and mp_size == 4:
+
+        def blocks(parts):
+            stacked = jnp.concatenate(parts, axis=0).astype(BF16)
+            return jnp.swapaxes(stacked.reshape(-1, dp_size, lane_block), 0, 1)
+
+        tables = jnp.concatenate([grad_table_attn, grad_table_ffn], axis=0)
+        tables = jnp.swapaxes(tables.reshape(-1, dp_size, lane_block), 0, 1)
+        grad_attn, grad_ffn, tables = reduce_grads(
+            blocks([grad_qkv[:, 0], grad_qkv[:, 1], grad_qkv[:, 2], grad_out_proj]),
+            blocks([grad_up, grad_down]),
+            tables,
+            dp_size,
+        )
+        grad_attn = grad_attn.reshape(w_attn.shape[0], 4, lane_block)
+        grad_ffn = grad_ffn.reshape(w_ffn.shape[0], 2, lane_block)
+        tables = lax.psum_scatter(
+            tables.reshape(2, ada_attn.shape[0], 2, lane_block),
+            "mp",
+            scatter_dimension=3,
+            tiled=True,
+        )
+        return (output, grad_tokens, grad_attn, grad_ffn, tables[0], tables[1])
     grad_attn_local = jnp.concatenate([grad_qkv, grad_out_proj[:, None, :]], axis=1)
     grad_ffn_local = jnp.stack([grad_up, grad_down], axis=1)
     grad_attn, grad_ffn = (

time: 904 us -> 632 us (0.70)
  waiting for transfers between devices: 625 us -> 267 us
  Pallas kernels: 0 us -> 94.7 us
    unnamed x17 -> x12, waiting for transfers between devices: 336 us -> 21 us
    pallas_call x0 -> x1, Pallas kernels: none -> 94.7 us  [reduce_grads(): pl.pallas_call(functools.partial(grads_kernel, z_size, 4), out_shape=(jax...]
    reduce_scatter x1 -> x0, waiting for transfers between devices: 54.6 us -> none  [shards(): lax.psum_scatter(grad_attn_local.astype(jnp.bfloat16), 'dp', scatter_dime...]
    reduce_scatter x1, waiting for transfers between devices: 13.2 us -> 52.1 us  [shards(): lax.psum_scatter(jnp.einsum('kr,kpc->rpc', picker, prompt_grad, precision...]
    reduce_scatter x1, waiting for transfers between devices: 28.7 us -> 0.01 us  [shards(): lax.psum_scatter(jnp.einsum('tsj,jsd->td', d_qkv, w_qkv, preferred_elemen...]
    unnamed x101 -> x102, local copies, waits for them, and re-layouts: 45.2 us -> 22.6 us
    concatenate x0 -> x6, local copies, waits for them, and re-layouts: none -> 12.6 us  [the longest x5 12.5 us: blocks(): stacked = jnp.concatenate(parts, axis=0).astype(BF16)]
  transfers between devices with their start and end apart: 14 -> 11, of which waited for: 14 -> 10; matrix products, arithmetic and copies ran while one was open for 16% -> 17% of each run, Pallas kernels for 0% -> 0%
where the time goes in v1:
time: 632 us; the launch traced here: 628 us
  waiting for transfers between devices  267 us (42%)
  matrix products  122 us (19%)
  Pallas kernels  94.7 us (15%)
  local copies, waits for them, and re-layouts  69.5 us (11%)
  other arithmetic  57 us (9%)
  between operations  16.9 us (3%)
    pallas_call x1, Pallas kernels, reduce_grads(): pl.pallas_call(functools.partial(grads_kernel, z_size, 4), out_shape=(jax...  94.7 us
    reduce_scatter x1, waiting for transfers between devices, shards(): lax.psum_scatter(jnp.einsum('kr,kpc->rpc', picker, prompt_grad, precision...  52.1 us
    all_gather x1, waiting for transfers between devices, shards(): shard_rows = lax.all_gather(windows, 'dp', axis=0, tiled=True)  42.3 us
    reduce_scatter x1, waiting for transfers between devices, shards(): lax.psum_scatter(jnp.dot(activated, w_down, preferred_element_type=jnp.fl...  32.5 us
    reduce_scatter x1, waiting for transfers between devices, shards(): lax.psum_scatter(jnp.dot(attn_flat, w_out, preferred_element_type=jnp.flo...  29 us
    dot_general x3, matrix products, inner_cols(): lax.dot_general(left, right, (((1,), (1,)), ((), ())), preferred_element_...  27.7 us
    reduce_scatter x1, waiting for transfers between devices, shards(): lax.psum_scatter(jnp.dot(d_up, w_up, preferred_element_type=jnp.float32)....  24.8 us
    all_gather x1, waiting for transfers between devices, shards(): normed_attn_full = lax.all_gather(normed_attn, 'mp', axis=0, tiled=True)  22.8 us
  transfers between devices with their start and end apart: 11, of which 10 were waited for; matrix products, arithmetic and copies ran while one was open for 17% of the time, Pallas kernels for 0%

profile of v1, /device:TPU:0, one launch (start us, length us, event | category | flops | bytes accessed | tf_op | source)
XLA Modules:
  0.0 627.8 jit_solution(18370476319056807431)
XLA Ops:
  18.6 22.8 %all-gather.6.cloned.1.call-done = bf16[1024,1024]{1,0:T(8,128)(2,1)} async-done(((bf16[256,1024]{1,0:T(8,128)(2,1)}), bf16[1024,1024]{1,0:T(8,128)(2,1)}) %all-gather.6.cloned.1.call-update) | async-done | bytes 2097168 | tf_op jit(solution)/shard_map/all_gather | solution.py:337
  41.4 4.3 fusion.38
  47.1 3.7 slice.124
  54.2 42.3 %all-gather.8.cloned.1.call-done = bf16[8,256,512]{2,1,0:T(8,128)(2,1)} async-done(((bf16[1,256,512]{2,1,0:T(8,128)(2,1)}), bf16[8,256,512]{2,1,0:T(8,128)(2,1)}) %all-gather.8.cloned.1.call-update) | async-done | bytes 2097168 | tf_op jit(solution)/shard_map/all_gather | solution.py:347
  96.5 3.6 fusion.23
  104.1 3.8 exponential_reduce_fusion
  111.1 8.9 %fusion.41 = bf16[4,64,1024]{2,1,0:T(8,128)(2,1)S(1)} fusion(f32[4,1024,1280]{2,1,0:T(8,128)} %copy-done, f32[4,1024]{1,0:T(4,128)S(1)} %log_add_fusion, bf16[256,4,64]{0,2,1:T(8,128)(2,1)S(1)} %bitcast.228, bf16[1024,4,64]{0,2,1:T(8,128)(2,1)S(1)} %bitcast.209), kind=kOutput, calls=%fused_computation.77 | convolution fusion | flops 683147264 | bytes 22167552 | tf_op jit(solution)/shard_map/while/body/eval_jaxpr/hqk,khd->qhd/dot_general | solution.py:74
  124.1 29.0 %reduce-scatter.9.cloned.1.call-done = bf16[256,1024]{1,0:T(8,128)(2,1)} async-done(((bf16[1024,1024]{1,0:T(8,128)(2,1)}), bf16[256,1024]{1,0:T(8,128)(2,1)}) %reduce-scatter.9.cloned.1.call-update) | async-done | bytes 524304 | tf_op jit(solution)/shard_map/reduce_scatter | solution.py:361
  158.7 9.9 %fusion.100 = (bf16[1024,1,1024]{2,1,0:T(2,128)(2,1)}, bf16[1024,1,1024]{2,1,0:T(2,128)(2,1)}) fusion(bf16[1024,2,1024]{2,1,0:T(2,128)(2,1)} %param.15), kind=kLoop, calls=%fused_computation.180 | loop fusion | bytes 8388608 | tf_op jit(solution)/shard_map/slice | solution.py:370
  168.6 12.0 %all-gather.10.cloned.1.call-done = bf16[1024,1024]{1,0:T(8,128)(2,1)} async-done(((bf16[256,1024]{1,0:T(8,128)(2,1)}), bf16[1024,1024]{1,0:T(8,128)(2,1)}) %all-gather.10.cloned.1.call-update) | async-done | bytes 2097168 | tf_op jit(solution)/shard_map/all_gather | solution.py:368
  180.6 16.2 %multiply_convert_fusion.2 = (bf16[1024,1024]{1,0:T(8,128)(2,1)}, f32[1024,1024]{1,0:T(8,128)}, f32[1024,1024]{1,0:T(8,128)}) fusion(bf16[1024,1024]{1,0:T(8,128)(2,1)} %all-gather.10.cloned.1.call-done, bf16[1024,1,1024]{2,1,0:T(2,128)(2,1)} %get-tuple-element.124), kind=kOutput, calls=%fused_computation.12 | convolution fusion | flops 2215641088 | bytes 14680064 | tf_op jit(solution)/shard_map/dot_general | solution.py:53
  196.8 7.9 %all-gather.12.cloned.1.call-done = bf16[1024,1024]{1,0:T(8,128)(2,1)} async-done(((bf16[256,1024]{1,0:T(8,128)(2,1)}), bf16[1024,1024]{1,0:T(8,128)(2,1)}) %all-gather.12.cloned.1.call-update) | async-done | bytes 2097168 | tf_op jit(solution)/shard_map/all_gather | solution.py:382
  204.7 8.9 %add_convert_fusion = bf16[1024,1024]{1,0:T(8,128)(2,1)S(1)} fusion(f32[1024,1024]{1,0:T(8,128)} %get-tuple-element.122, f32[1024,1024]{1,0:T(8,128)} %get-tuple-element.144, bf16[1024,1024]{1,0:T(8,128)(2,1)} %all-gather.12.cloned.1.call-done, bf16[1024,1,1024]{2,1,0:T(2,128)(2,1)} %get-tuple-element.123), kind=kOutput, calls=%fused_computation.11 | convolution fusion | flops 2162163712 | bytes 14680064 | tf_op jit(solution)/shard_map/dot_general | solution.py:53
  214.9 3.8 convolution_convert_fusion.2
  218.8 6.7 %convolution_convert_fusion.3 = bf16[1024,1024]{1,0:T(8,128)(2,1)} fusion(bf16[1024,1024]{1,0:T(8,128)(2,1)} %get-tuple-element.121, bf16[1024,1,1024]{2,1,0:T(2,128)(2,1)} %get-tuple-element.123), kind=kOutput, calls=%fused_computation.54 | convolution fusion | flops 2148532224 | bytes 6291456 | tf_op jit(solution)/shard_map/dot_general | solution.py:376
  225.5 24.8 %reduce-scatter.13.cloned.1.call-done = bf16[256,1024]{1,0:T(8,128)(2,1)} async-done(((bf16[1024,1024]{1,0:T(8,128)(2,1)}), bf16[256,1024]{1,0:T(8,128)(2,1)}) %reduce-scatter.13.cloned.1.call-update) | async-done | bytes 524304 | tf_op jit(solution)/shard_map/reduce_scatter | solution.py:388
  251.8 32.5 %reduce-scatter.11.cloned.1.call-done = bf16[256,1024]{1,0:T(8,128)(2,1)} async-done(((bf16[1024,1024]{1,0:T(8,128)(2,1)}), bf16[256,1024]{1,0:T(8,128)(2,1)}) %reduce-scatter.11.cloned.1.call-update) | async-done | bytes 524304 | tf_op jit(solution)/shard_map/reduce_scatter | solution.py:375
  290.0 22.0 %all-gather.14.cloned.1.call-done = bf16[1024,1024]{1,0:T(8,128)(2,1)} async-done(((bf16[256,1024]{1,0:T(8,128)(2,1)}), bf16[1024,1024]{1,0:T(8,128)(2,1)}) %all-gather.14.cloned.1.call-update) | async-done | bytes 2097168 | tf_op jit(solution)/shard_map/all_gather | solution.py:401
  314.7 9.0 %fusion.11 = f32[1280,4,64]{0,2,1:T(8,128)S(1)} fusion(bf16[1024,4,64]{0,2,1:T(8,128)(2,1)S(1)} %bitcast.213, f32[4,1024,1280]{2,1,0:T(8,128)} %copy-done, f32[4,1024]{1,0:T(4,128)S(1)} %log_add_fusion), kind=kOutput, calls=%fused_computation.34 | convolution fusion | flops 681574400 | bytes 22822912 | tf_op jit(solution)/shard_map/while/body/eval_jaxpr/hqk,qhd->khd/dot_general | solution.py:85
  323.7 13.7 %multiply_reduce_fusion = (f32[4,1024]{1,0:T(4,128)S(1)}, f32[4,1024,1280]{2,1,0:T(8,128)}) fusion(f32[4,1024,1280]{2,1,0:T(8,128)} %copy-done, f32[4,1024]{1,0:T(4,128)S(1)} %log_add_fusion, bf16[1024,4,64]{0,2,1:T(8,128)(2,1)S(1)} %bitcast.214, bf16[256,4,64]{0,2,1:T(8,128)(2,1)S(1)} %bitcast.229, bf16[1024,4,64]{0,2,1:T(8,128)(2,1)S(1)} %bitcast.210), kind=kOutput, calls=%fused_computation.1 | convolution fusion | flops 688123904 | bytes 43155456 | tf_op jit(solution)/shard_map/while/body/eval_jaxpr/qhd,khd->hqk/dot_general | solution.py:86
  337.4 14.2 %multiply_convert_fusion = bf16[4,1024,1280]{2,1,0:T(8,128)(2,1)S(1)} fusion(f32[4,1024,1280]{2,1,0:T(8,128)} %get-tuple-element.146, f32[4,1024,1280]{2,1,0:T(8,128)} %copy-done, f32[4,1024]{1,0:T(4,128)S(1)} %get-tuple-element.145, f32[4,1024]{1,0:T(4,128)S(1)} %log_add_fusion), kind=kLoop, calls=%fused_computation | loop fusion | flops 20971520 | bytes 52461568 | tf_op jit(solution)/shard_map/while/body/eval_jaxpr/convert_element_type | solution.py:88
  364.3 7.4 %fusion.44 = bf16[4,64,1024]{2,1,0:T(8,128)(2,1)S(1)} fusion(bf16[4,1024,1280]{2,1,0:T(8,128)(2,1)} %copy-done.1, bf16[256,4,64]{0,2,1:T(8,128)(2,1)S(1)} %bitcast.227, bf16[1024,4,64]{0,2,1:T(8,128)(2,1)S(1)} %bitcast.208), kind=kOutput, calls=%fused_computation.80 | convolution fusion | flops 672923648 | bytes 11665408 | tf_op jit(solution)/shard_map/while/body/eval_jaxpr/hqk,khd->qhd/dot_general | solution.py:89
  374.8 52.1 %reduce-scatter.15.cloned.1.call-done = bf16[1,256,512]{2,1,0:T(8,128)(2,1)} async-done(((bf16[8,256,512]{2,1,0:T(8,128)(2,1)}), bf16[1,256,512]{2,1,0:T(8,128)(2,1)}) %reduce-scatter.15.cloned.1.call-update) | async-done | bytes 262160 | tf_op jit(solution)/shard_map/reduce_scatter | solution.py:418
  429.3 3.4 scatter.4
  435.0 5.1 bitcast_convert_fusion
  440.2 5.3 convolution_convert_fusion.1
  448.8 6.0 convolution_convert_fusion
  454.7 4.0 copy.78
  458.7 3.9 maximum_bitcast_fusion.gf
  472.0 3.8 fusion.35
  495.0 94.7 %shard_map.154 = (f32[1024,128]{1,0:T(8,128)}, f32[2048,128]{1,0:T(8,128)}, f32[32,128]{1,0:T(8,128)}) custom-call(bf16[8,1024,128]{2,1,0:T(8,128)(2,1)} %maximum_bitcast_fusion.1.ga, bf16[8,2048,128]{2,1,0:T(8,128)(2,1)} %maximum_bitcast_fusion.gf, f32[8,32,128]{2,1,0:T(8,128)} %bitcast.233), custom_call_target="tpu_custom_call" | custom-call | tf_op jit(solution)/shard_map/pallas_call | solution.py:279
  595.3 20.3 %reduce-scatter.19.cloned.1.call-done = f32[32,32]{1,0:T(8,128)} async-done(((f32[128,32]{1,0:T(8,128)}), f32[32,32]{1,0:T(8,128)}) %reduce-scatter.19.cloned.1.call-update) | async-done | bytes 4112
  (210 shorter events, 105.0 us)
Async XLA Ops:
  7.2 8.9 %copy-start.44 = (s32[8]{0:T(128)S(1)}, s32[8]{0:T(128)}, u32[]{:S(2)}) copy-start(s32[8]{0:T(128)} %param.21) | copy-start | bytes 100
  7.2 34.2 %all-gather.6.cloned.1.call-start = ((), (), s32[]{:S(2)}) async-start(), calls=%async_computation.6 | async-start | bytes 2621440 | tf_op jit(solution)/shard_map/all_gather | solution.py:337
  8.4 37.2 %copy-start.31 = (f32[256]{0:T(256)}, f32[256]{0:T(256)S(1)}, u32[]{:S(2)}) copy-start(f32[256]{0:T(256)S(1)} %broadcast_multiply_fusion.1) | copy-start | bytes 3076
  9.8 35.9 %copy-start.37 = (f32[256]{0:T(256)}, f32[256]{0:T(256)S(1)}, u32[]{:S(2)}) copy-start(f32[256]{0:T(256)S(1)} %fusion.50) | copy-start | bytes 3076
  9.8 35.9 %copy-start.35 = (f32[256]{0:T(256)}, f32[256]{0:T(256)S(1)}, u32[]{:S(2)}) copy-start(f32[256]{0:T(256)S(1)} %fusion.84) | copy-start | bytes 3076
  10.6 112.5 %copy-start.33 = (s32[256]{0:T(256)}, s32[256]{0:T(256)S(1)}, u32[]{:S(2)}) copy-start(s32[256]{0:T(256)S(1)} %select_reduce_fusion) | copy-start | bytes 3076
  16.0 80.5 %all-gather.8.cloned.1.call-start = ((), (), s32[]{:S(2)}) async-start(), calls=%async_computation.7 | async-start | bytes 2359296 | tf_op jit(solution)/shard_map/all_gather | solution.py:347
  46.9 106.2 %reduce-scatter.9.cloned.1.call-start = ((), (), s32[]{:S(2)}) async-start(), calls=%async_computation.8 | async-start | bytes 2621440 | tf_op jit(solution)/shard_map/reduce_scatter | solution.py:361
  54.2 49.9 %copy-start.8 = (bf16[1024,1,256]{0,2,1:T(8,128)(2,1)}, bf16[1024,1,256]{0,2,1:T(8,128)(2,1)S(1)}, u32[]{:S(2)}) copy-start(bf16[1024,1,256]{0,2,1:T(8,128)(2,1)S(1)} %get-tuple-element.131) | copy-start | bytes 1572868
  54.2 49.9 %copy-start.12 = (bf16[1024,1,256]{0,2,1:T(8,128)(2,1)}, bf16[1024,1,256]{0,2,1:T(8,128)(2,1)S(1)}, u32[]{:S(2)}) copy-start(bf16[1024,1,256]{0,2,1:T(8,128)(2,1)S(1)} %get-tuple-element.130) | copy-start | bytes 1572868
  54.2 56.9 %copy-start.14 = (bf16[1024,1,256]{0,2,1:T(8,128)(2,1)}, bf16[1024,1,256]{0,2,1:T(8,128)(2,1)S(1)}, u32[]{:S(2)}) copy-start(bf16[1024,1,256]{0,2,1:T(8,128)(2,1)S(1)} %get-tuple-element.129) | copy-start | bytes 1572868
  111.1 9.7 %copy-start.23 = (bf16[256,1,1024]{2,1,0:T(2,128)(2,1)S(1)}, bf16[256,1,1024]{2,1,0:T(2,128)(2,1)}, u32[]{:S(2)}) copy-start(bf16[256,1,1024]{2,1,0:T(2,128)(2,1)} %slice.124) | copy-start | bytes 1572868
  120.0 33.0 %copy-start.2 = (bf16[256,1024]{1,0:T(8,128)(2,1)S(1)}, bf16[256,1024]{1,0:T(8,128)(2,1)}, u32[]{:S(2)}) copy-start(bf16[256,1024]{1,0:T(8,128)(2,1)} %param.13) | copy-start | bytes 1572868
  123.0 57.6 %all-gather.10.cloned.1.call-start = ((), (), s32[]{:S(2)}) async-start(), calls=%async_computation.9 | async-start | bytes 2621440 | tf_op jit(solution)/shard_map/all_gather | solution.py:368
  157.8 46.9 %all-gather.12.cloned.1.call-start = ((), (), s32[]{:S(2)}) async-start(), calls=%async_computation.11 | async-start | bytes 2621440 | tf_op jit(solution)/shard_map/all_gather | solution.py:382
  158.4 91.9 %reduce-scatter.13.cloned.1.call-start = ((), (), s32[]{:S(2)}) async-start(), calls=%async_computation.12 | async-start | bytes 2621440 | tf_op jit(solution)/shard_map/reduce_scatter | solution.py:388
  204.7 10.2 %copy-start.22 = (bf16[1024,1,1024]{2,1,0:T(2,128)(2,1)S(1)}, bf16[1024,1,1024]{2,1,0:T(2,128)(2,1)}, u32[]{:S(2)}) copy-start(bf16[1024,1,1024]{2,1,0:T(2,128)(2,1)} %get-tuple-element.124) | copy-start | bytes 6291460
  218.7 65.5 %reduce-scatter.11.cloned.1.call-start = ((), (), s32[]{:S(2)}) async-start(), calls=%async_computation.10 | async-start | bytes 2621440 | tf_op jit(solution)/shard_map/reduce_scatter | solution.py:375
  218.8 31.5 %copy-start.5 = (bf16[256,1024]{1,0:T(8,128)(2,1)S(1)}, bf16[256,1024]{1,0:T(8,128)(2,1)}, u32[]{:S(2)}) copy-start(bf16[256,1024]{1,0:T(8,128)(2,1)} %reduce-scatter.9.cloned.1.call-done) | copy-start | bytes 1572868
  225.5 86.6 %all-gather.14.cloned.1.call-start = ((), (), s32[]{:S(2)}) async-start(), calls=%async_computation.13 | async-start | bytes 2621440 | tf_op jit(solution)/shard_map/all_gather | solution.py:401
  289.3 137.6 %reduce-scatter.15.cloned.1.call-start = ((), (), s32[]{:S(2)}) async-start(), calls=%async_computation.14 | async-start | bytes 2359296 | tf_op jit(solution)/shard_map/reduce_scatter | solution.py:418
  314.7 9.0 %copy-start.15 = (bf16[1024,1,256]{0,2,1:T(8,128)(2,1)S(1)}, bf16[1024,1,256]{0,2,1:T(8,128)(2,1)}, u32[]{:S(2)}) copy-start(bf16[1024,1,256]{0,2,1:T(8,128)(2,1)} %copy-done.14) | copy-start | bytes 1572868
  323.7 13.7 %copy-start.10 = (f32[1280,4,64]{0,2,1:T(8,128)}, f32[1280,4,64]{0,2,1:T(8,128)S(1)}, u32[]{:S(2)}) copy-start(f32[1280,4,64]{0,2,1:T(8,128)S(1)} %fusion.11) | copy-start | bytes 3932164
  337.3 14.2 %copy-start.9 = (bf16[1024,1,256]{0,2,1:T(8,128)(2,1)S(1)}, bf16[1024,1,256]{0,2,1:T(8,128)(2,1)}, u32[]{:S(2)}) copy-start(bf16[1024,1,256]{0,2,1:T(8,128)(2,1)} %copy-done.8) | copy-start | bytes 1572868
  358.9 126.3 %reduce-scatter.17.cloned.1.call-start = ((), (), s32[]{:S(2)}) async-start(), calls=%async_computation.15 | async-start | bytes 2621440 | tf_op jit(solution)/shard_map/reduce_scatter | solution.py:444
  372.0 62.1 %copy-start.26 = (bf16[1024,1,256]{2,0,1:T(8,128)(2,1)}, bf16[1024,1,256]{2,0,1:T(8,128)(2,1)S(1)}, u32[]{:S(2)}) copy-start(bf16[1024,1,256]{2,0,1:T(8,128)(2,1)S(1)} %copy.71) | copy-start | bytes 1572868
  440.1 175.5 %reduce-scatter.19.cloned.1.call-start = ((), (), s32[]{:S(2)}) async-start(), calls=%async_computation.16 | async-start | bytes 81920
  476.9 8.3 %copy-start.32 = (f32[256]{0:T(256)S(1)}, f32[256]{0:T(256)}, u32[]{:S(2)}) copy-start(f32[256]{0:T(256)} %copy-done.31) | copy-start | bytes 3076
  495.0 99.2 %copy-start.7 = (f32[256,1024]{1,0:T(8,128)S(1)}, f32[256,1024]{1,0:T(8,128)}, u32[]{:S(2)}) copy-start(f32[256,1024]{1,0:T(8,128)} %copy-done.6) | copy-start | bytes 3145732
  495.0 99.2 %copy-start.19 = (bf16[256,1024]{1,0:T(8,128)(2,1)S(1)}, bf16[256,1024]{1,0:T(8,128)(2,1)}, u32[]{:S(2)}) copy-start(bf16[256,1024]{1,0:T(8,128)(2,1)} %param.23) | copy-start | bytes 1572868
  495.0 99.2 %copy-start.21 = (f32[256,1024]{1,0:T(8,128)S(1)}, f32[256,1024]{1,0:T(8,128)}, u32[]{:S(2)}) copy-start(f32[256,1024]{1,0:T(8,128)} %get-tuple-element.118) | copy-start | bytes 3145732
  589.7 28.2 %copy-start.27 = (f32[1024,128]{1,0:T(8,128)S(1)}, f32[1024,128]{1,0:T(8,128)}, u32[]{:S(2)}) copy-start(f32[1024,128]{1,0:T(8,128)} %get-tuple-element.76) | copy-start | bytes 1572868
  (28 other events, 115.7 us)
Sparse Core Ops, SparseCore 0:
  16.1 25.2 all-gather.5
  47.0 49.4 all-gather.7
  123.1 29.8 reduce-scatter.8
  158.0 22.5 all-gather.9
  182.1 22.5 all-gather.11
  218.8 31.4 reduce-scatter.12
  252.8 31.3 reduce-scatter.10
  289.4 22.5 all-gather.13
  359.1 67.8 reduce-scatter.14
  440.2 30.4 reduce-scatter.16
  594.3 21.2 reduce-scatter.18

commit v2 on v0

--- a/solution.py
+++ b/solution.py
@@ -1,6 +1,11 @@
+import collections
+import functools
+
 import jax
 import jax.numpy as jnp
 from jax import lax
+from jax.experimental import pallas as pl
+from jax.experimental.pallas import tpu as pltpu
 from jax.sharding import PartitionSpec as P
 
 HD = 64
@@ -86,6 +91,841 @@
     ) * HD ** (-0.5)
     own_len = queries.shape[0]
     return (d_queries, d_keys[:own_len], d_values[:own_len], d_keys[own_len:], d_values[own_len:])
+
+
+MESH = pl.DeviceIdType.MESH
+F32 = jnp.float32
+BF16 = jnp.bfloat16
+LANES = 128
+
+
+def dot(left, right, left_dim=1, right_dim=0):
+    return lax.dot_general(
+        left, right, (((left_dim,), (right_dim,)), ((), ())), preferred_element_type=F32
+    )
+
+
+class Links:
+    def __init__(self, z_size, send_sem, recv_sem):
+        self.dp = lax.axis_index("dp")
+        self.mp = lax.axis_index("mp")
+        self.z_size = z_size
+        self.y = lax.rem(self.dp, 2)
+        self.z = self.dp // 2
+        self.core = lax.rem(self.mp, 2)
+        self.x = self.mp // 2
+        self.sib = (self.dp, self.mp + 1 - 2 * self.core)
+        self.xpeer = (self.dp, self.mp + 2 - 4 * self.x)
+        self.ypeer = (self.dp + 1 - 2 * self.y, self.mp)
+        self.right = (self.dp + 2, self.mp)
+        self.left = (self.dp - 2, self.mp)
+        self.send_sem = send_sem
+        self.recv_sem = recv_sem
+        self.used = 0
+        self.sent = []
+        self.pair_sends = {}
+
+    def take(self, count=1):
+        first = self.used
+        self.used += count
+        return first
+
+    def copy(self, src, dst, number, device):
+        return pltpu.make_async_remote_copy(
+            src_ref=src,
+            dst_ref=dst,
+            send_sem=self.send_sem.at[number],
+            recv_sem=self.recv_sem.at[number],
+            device_id=device,
+            device_id_type=MESH,
+        )
+
+    def swap(self, src, dst, device):
+        made = self.copy(src, dst, self.take(), device)
+        self.sent.append(made)
+        return made
+
+    def finish(self, made=None):
+        for one in list(self.sent):
+            if made is None or one is made:
+                one.wait_send()
+        self.sent = [one for one in self.sent if made is not None and one is not made]
+
+    def barrier(self):
+        bar = pltpu.get_barrier_semaphore()
+        for device in (self.sib, self.xpeer, self.ypeer):
+            pl.semaphore_signal(bar, inc=1, device_id=device, device_id_type=MESH)
+
+        @pl.when(self.z > 0)
+        def _():
+            pl.semaphore_signal(bar, inc=1, device_id=self.left, device_id_type=MESH)
+
+        @pl.when(self.z < self.z_size - 1)
+        def _():
+            pl.semaphore_signal(bar, inc=1, device_id=self.right, device_id_type=MESH)
+
+        inner = (self.z > 0).astype(jnp.int32) + (self.z < self.z_size - 1).astype(jnp.int32)
+        pl.semaphore_wait(bar, 3 + inner)
+
+
+class LineReduce:
+    def __init__(self, links, held, passing):
+        self.setup(links, held, passing)
+
+    def setup(self, links, held, passing):
+        self.k = links
+        self.held, self.passing = held, passing
+        self.nr = links.take(links.z_size)
+        self.nl = links.take(links.z_size)
+
+    def order(self):
+        n = self.k.z_size
+        return [n - 1, 0] + list(range(1, n - 1))
+
+    def z_copy(self, d, rightward):
+        k = self.k
+        if rightward:
+            return k.copy(self.held.at[d], self.passing.at[d], self.nr + d, k.right)
+        slot = jnp.where(k.z - 1 == d, k.z_size, d)
+        return k.copy(self.held.at[d], self.passing.at[slot], self.nl + d, k.left)
+
+    def add(self, d):
+        total = self.held[d].astype(F32) + self.passing[d].astype(F32)
+        self.held[d] = total.astype(self.held.dtype)
+
+    def move(self, d):
+        k = self.k
+
+        @pl.when(k.z < d)
+        def _():
+            @pl.when(k.z > 0)
+            def _():
+                self.z_copy(d, True).wait_recv()
+                self.add(d)
+
+            self.z_copy(d, True).start()
+
+        @pl.when(k.z > d)
+        def _():
+            @pl.when(k.z < k.z_size - 1)
+            def _():
+                self.z_copy(d, False).wait_recv()
+                self.add(d)
+
+            self.z_copy(d, False).start()
+
+    def finish(self, store):
+        k = self.k
+        n = k.z_size
+
+        @pl.when(k.z > 0)
+        def _():
+            k.copy(self.held.at[k.z], self.passing.at[k.z], self.nr + k.z, k.left).wait_recv()
+
+        @pl.when(k.z < n - 1)
+        def _():
+            k.copy(self.held.at[k.z], self.passing.at[n], self.nl + k.z, k.right).wait_recv()
+
+        total = self.held[k.z].astype(F32)
+        from_left = jnp.where(k.z > 0, self.passing[k.z].astype(F32), 0.0)
+        from_right = jnp.where(k.z < n - 1, self.passing[n].astype(F32), 0.0)
+        store(total + from_left + from_right)
+
+    def wait_sends(self):
+        k = self.k
+        for d in range(k.z_size):
+
+            @pl.when(k.z < d)
+            def _(d=d):
+                self.z_copy(d, True).wait_send()
+
+            @pl.when(k.z > d)
+            def _(d=d):
+                self.z_copy(d, False).wait_send()
+
+
+class GridReduce(LineReduce):
+    def __init__(self, links, local, held, passing):
+        self.setup(links, held, passing)
+        self.local = local
+        self.ny = links.take(links.z_size)
+
+    def y_copy(self, d):
+        k = self.k
+        other = 2 * d + 1 - k.y
+        return k.copy(self.local.at[other], self.held.at[d], self.ny + d, k.ypeer)
+
+    def send_y(self):
+        for d in self.order():
+            self.y_copy(d).start()
+
+    def merge_y(self, d):
+        self.y_copy(d).wait_recv()
+        total = self.local[2 * d + self.k.y].astype(F32) + self.held[d].astype(F32)
+        self.held[d] = total.astype(self.held.dtype)
+
+    def serve(self):
+        for d in self.order():
+            self.merge_y(d)
+            self.move(d)
+
+    def wait_y(self):
+        for d in range(self.k.z_size):
+            self.y_copy(d).wait_send()
+
+
+class LineGather:
+    def __init__(self, links, slots):
+        self.k = links
+        self.slots = slots
+        self.nr = links.take(links.z_size)
+        self.nl = links.take(links.z_size)
+
+    def z_copy(self, slot, rightward):
+        k = self.k
+        number = (self.nr if rightward else self.nl) + slot
+        place = self.slots.at[slot]
+        return k.copy(place, place, number, k.right if rightward else k.left)
+
+    def start(self):
+        k = self.k
+
+        @pl.when(k.z < k.z_size - 1)
+        def _():
+            self.z_copy(k.z, True).start()
+
+        @pl.when(k.z > 0)
+        def _():
+            self.z_copy(k.z, False).start()
+
+    def serve(self, distance):
+        k = self.k
+
+        @pl.when(k.z >= distance)
+        def _():
+            self.z_copy(k.z - distance, True).wait_recv()
+
+            @pl.when(k.z < k.z_size - 1)
+            def _():
+                self.z_copy(k.z - distance, True).start()
+
+        @pl.when(k.z + distance < k.z_size)
+        def _():
+            self.z_copy(k.z + distance, False).wait_recv()
+
+            @pl.when(k.z > 0)
+            def _():
+                self.z_copy(k.z + distance, False).start()
+
+    def wait_sends(self):
+        k = self.k
+        for slot in range(k.z_size):
+
+            @pl.when(jnp.logical_and(k.z >= slot, k.z < k.z_size - 1))
+            def _(slot=slot):
+                self.z_copy(slot, True).wait_send()
+
+            @pl.when(jnp.logical_and(k.z <= slot, k.z > 0))
+            def _(slot=slot):
+                self.z_copy(slot, False).wait_send()
+
+
+class Exchange:
+    def __init__(self, links, pair_out, pair_in, x_out, x_in):
+        self.k = links
+        self.pair_out, self.pair_in, self.x_out, self.x_in = pair_out, pair_in, x_out, x_in
+        self.pair = {}
+        self.along_x = {}
+
+    def give(self, r, term, slot=None):
+        slot = r if slot is None else slot
+        if slot in self.k.pair_sends:
+            self.k.finish(self.k.pair_sends[slot])
+        self.pair_out[slot] = term.astype(BF16)
+        made = self.k.swap(self.pair_out.at[slot], self.pair_in.at[slot], self.k.sib)
+        made.start()
+        self.k.pair_sends[slot] = made
+        self.pair[r] = (made, slot)
+
+    def pair_sum(self, r, term):
+        made, slot = self.pair[r]
+        made.wait_recv()
+        return term + self.pair_in[slot].astype(F32)
+
+    def send_x(self, r, total):
+        self.x_out[r] = total.astype(BF16)
+        made = self.k.swap(self.x_out.at[r], self.x_in.at[r], self.k.xpeer)
+        made.start()
+        self.along_x[r] = made
+
+    def total(self, r):
+        self.along_x[r].wait_recv()
+        return self.x_out[r].astype(F32) + self.x_in[r].astype(F32)
+
+
+class Settle:
+    def __init__(self, exchange, shards, x_out, x_in, term):
+        k = exchange.k
+        own, sib, across, diag = shards
+        exchange.give(2, term(diag), 0)
+        x_out[...] = exchange.pair_sum(2, term(across)).astype(BF16)
+        self.along_x = k.swap(x_out, x_in, k.xpeer)
+        self.along_x.start()
+        self.x_in = x_in
+        exchange.give(3, term(sib), 1)
+        self.kept = exchange.pair_sum(3, term(own))
+
+    def total(self, kept):
+        self.along_x.wait_recv()
+        return kept + self.x_in[...].astype(F32)
+
+
+def normalize(values):
+    center = values - jnp.mean(values, axis=1, keepdims=True)
+    spread = jnp.mean(center * center, axis=1, keepdims=True)
+    scale = lax.rsqrt(spread + epsilon)
+    return center * scale, scale
+
+
+def norm_back(values, table, d_normed):
+    normed, scale = normalize(values)
+    dz = (1.0 + table[0:1, :]) * d_normed
+    both = jnp.mean(dz * normed, axis=1, keepdims=True)
+    d_values = (dz - jnp.mean(dz, axis=1, keepdims=True) - normed * both) * scale
+    d_gain = jnp.sum(d_normed * normed, axis=0, keepdims=True)
+    d_shift = jnp.sum(d_normed, axis=0, keepdims=True)
+    return d_values, d_gain, d_shift
+
+
+def layer_kernel(names, z_size, *refs):
+    held = dict(zip(names, refs))
+    held.update(
+        d_mixed=held["act"],
+        d_query=held["mixed"],
+        d_branch=held["normed_ffn"],
+        far_held=held["windows"],
+        d_query_low=held["attn_t"],
+        d_keys_low=held["keys_t"],
+        d_values_low=held["values_t"],
+        g_attn=held["g_down"],
+    )
+    n = collections.namedtuple("Buffers", held)(**held)
+    k = Links(z_size, n.send_sem, n.recv_sem)
+    mp_size, block, width = n.normed.shape
+    seq = mp_size * block
+    heads_wide = n.wa.shape[1]
+    hidden = n.wf.shape[1]
+    heads = heads_wide // HD
+    q_wide = heads * block
+    tile = block
+    far = mp_size
+    own_shard = 2 * k.x + k.core
+    sib_shard = 2 * k.x + 1 - k.core
+    x_shard = 2 * (1 - k.x) + k.core
+    diag_shard = 2 * (1 - k.x) + 1 - k.core
+    shards = (own_shard, sib_shard, x_shard, diag_shard)
+
+    def mine(r):
+        return 2 * r + k.core
+
+    def theirs(r):
+        return 2 * r + 1 - k.core
+
+    def span(i, size=tile):
+        return pl.ds(pl.multiple_of(i * size, size), size)
+
+    fetches = []
+
+    def fetch(src, dst):
+        made = pltpu.make_async_copy(src, dst, n.load_sem.at[len(fetches)])
+        made.start()
+        fetches.append(made)
+        return made
+
+    load_tokens = fetch(n.tokens, n.raw.at[k.x])
+    load_wa = fetch(n.w_attn, n.wa)
+    load_cot = fetch(n.cotangent, n.cot.at[own_shard])
+    load_wf = fetch(n.w_ffn, n.wf)
+
+    def partner_of(row):
+        begin, first, count = 0, 0, 1
+        for g in range(n.group_sizes.shape[0]):
+            size = n.group_sizes[g]
+            inside = jnp.logical_and(row >= begin, row < begin + size)
+            first = jnp.where(inside, begin, first)
+            count = jnp.where(inside, size, count)
+            begin = begin + size
+        step = lax.rem(n.partner_pick[row], jnp.maximum(count - 1, 1))
+        return jnp.clip(first + lax.rem(row - first + 1 + step, count), 0, 2 * z_size - 1)
+
+    k.barrier()
+    send_tokens = k.swap(n.tokens, n.raw.at[k.x], k.xpeer)
+    send_tokens.start()
+    cot_x = k.swap(n.cotangent, n.cot.at[own_shard], k.xpeer)
+    cot_x.start()
+    cot_sib = k.swap(n.cotangent, n.cot.at[own_shard], k.sib)
+    cot_sib.start()
+
+    code = n.codebook[k.dp]
+    start = n.prompt_start[k.dp]
+    partner = partner_of(k.dp)
+    other_partner = partner_of(k.dp + 1 - 2 * k.y)
+    part_z, part_y = partner // 2, lax.rem(partner, 2)
+    other_z, other_y = other_partner // 2, lax.rem(other_partner, 2)
+    far_len = n.prompt_len[partner]
+    table_attn = n.ada_attn[code]
+    table_ffn = n.ada_ffn[code]
+
+    def adapt(normed, table):
+        return ((1.0 + table[0:1, :]) * normed + table[1:2, :]).astype(BF16)
+
+    def project(s):
+        normed = n.normed[s]
+        query = (dot(normed, n.wa[0], 1, 1) * HD ** (-0.5)).astype(BF16)
+        lane = lax.broadcasted_iota(jnp.int32, (block, heads_wide), 1) // HD
+        for h in range(heads):
+            n.q4[s, h * block : (h + 1) * block, :] = jnp.where(lane == h, query, 0).astype(BF16)
+        for ref, turned, w in ((n.keys, n.keys_t, 1), (n.values, n.values_t, 2)):
+            made = dot(normed, n.wa[w], 1, 1)
+            ref[s] = made.astype(BF16)
+            turned[s] = made.T.astype(BF16)
+
+    load_tokens.wait()
+    n.normed[own_shard] = adapt(normalize(n.raw[k.x].astype(F32))[0], table_attn)
+    normed_own = k.swap(n.normed.at[own_shard], n.normed.at[own_shard], k.sib)
+    normed_own.start()
+    load_wa.wait()
+    normed_own.wait_recv()
+
+    def project_pair(first):
+        def body(i, carry):
+            project(first + i)
+            return carry
+
+        lax.fori_loop(0, 2, body, 0)
+
+    project_pair(2 * k.x)
+    send_tokens.wait_recv()
+    n.normed[x_shard] = adapt(normalize(n.raw[1 - k.x].astype(F32))[0], table_attn)
+    normed_x = k.swap(n.normed.at[x_shard], n.normed.at[x_shard], k.sib)
+    normed_x.start()
+    normed_x.wait_recv()
+    project_pair(2 * (1 - k.x))
+
+    all_keys = n.keys[0:mp_size].reshape(seq, heads_wide)
+    all_values = n.values[0:mp_size].reshape(seq, heads_wide)
+    from_row = lax.broadcasted_iota(jnp.int32, (block, seq), 1)
+    to_row = lax.broadcasted_iota(jnp.int32, (block, seq), 0)
+    window = (from_row == to_row + start).astype(F32).astype(BF16)
+    n.windows[k.z, 0:block] = dot(window, all_keys).astype(BF16)
+    n.windows[k.z, block : 2 * block] = dot(window, all_values).astype(BF16)
+    gather = LineGather(k, n.windows)
+    gather.start()
+
+    def attend_own(s, carry):
+        q4 = n.q4[s]
+        top = jnp.full((1, q_wide), -jnp.inf, F32)
+        for c in range(mp_size):
+            scores = dot(n.keys[c], q4, 1, 1)
+            n.wide[c] = scores
+            top = jnp.maximum(top, jnp.max(scores, axis=0, keepdims=True))
+        total = jnp.zeros((1, q_wide), F32)
+        for c in range(mp_size):
+            prob = jnp.exp(n.wide[c] - top)
+            total = total + jnp.sum(prob, axis=0, keepdims=True)
+            low = prob.astype(BF16)
+            for h in range(heads):
+                rows = slice(h * HD, (h + 1) * HD)
+                part = dot(n.values_t[c, rows, :], low[:, h * block : (h + 1) * block])
+                n.mixed[s, rows, :] = part if c == 0 else n.mixed[s, rows, :] + part
+        n.top[s] = top
+        n.total[s] = total
+        return carry
+
+    for s in range(mp_size):
+        attend_own_s = functools.partial(attend_own)
+        lax.fori_loop(s, s + 1, attend_own_s, 0)
+        if 0 < s < z_size:
+            gather.serve(s)
+    for distance in range(mp_size, z_size):
+        gather.serve(distance)
+
+    n.y_out[...] = n.windows[other_z]
+    y_window = k.swap(n.y_out, n.y_in, k.ypeer)
+    y_window.start()
+    cot_x.wait_recv()
+    cot_pass = k.swap(n.cot.at[x_shard], n.cot.at[x_shard], k.sib)
+    cot_pass.start()
+    y_window.wait_recv()
+    same_y = part_y == k.y
+    far_kv = jnp.where(same_y, n.windows[part_z].astype(F32), n.y_in[...].astype(F32))
+    n.keys[far] = far_kv[0:block].astype(BF16)
+    n.values[far] = far_kv[block:].astype(BF16)
+    n.keys_t[far] = far_kv[0:block].T.astype(BF16)
+    n.values_t[far] = far_kv[block:].T.astype(BF16)
+
+    def attend_far(s):
+        scores = dot(n.keys[far], n.q4[s], 1, 1)
+        slot = lax.broadcasted_iota(jnp.int32, scores.shape, 0)
+        scores = jnp.where(slot < far_len, scores, -1000000000.0)
+        top = jnp.maximum(n.top[s], jnp.max(scores, axis=0, keepdims=True))
+        scale = jnp.exp(n.top[s] - top)
+        prob = jnp.exp(scores - top)
+        total = n.total[s] * scale + jnp.sum(prob, axis=0, keepdims=True)
+        low = prob.astype(BF16)
+        for h in range(heads):
+            rows = slice(h * HD, (h + 1) * HD)
+            cols = slice(h * block, (h + 1) * block)
+            part = n.mixed[s, rows, :] * scale[:, cols] + dot(n.values_t[far, rows, :], low[:, cols])
+            n.attn_t[s, rows, :] = (part / total[:, cols]).astype(BF16)
+        n.log_total[s] = top + jnp.log(total)
+
+    def out_part(s):
+        attend_far(s)
+        return dot(n.attn_t[s], n.wa[3], 0, 0)
+
+    branch = Exchange(k, n.pair_out, n.pair_in, n.x_out, n.x_in)
+    for r in range(2):
+        branch.give(r, out_part(theirs(r)))
+        branch.send_x(r, branch.pair_sum(r, out_part(mine(r))))
+
+    back = Exchange(k, n.pair_out, n.pair_in, n.x_out2, n.x_in2)
+    load_cot.wait()
+    load_wf.wait()
+    cot_sib.wait_recv()
+    cot_pass.wait_recv()
+
+    def hidden_part(s):
+        normed = n.normed_ffn[s]
+        cot = n.cot[s]
+
+        def body(i, carry):
+            cols = span(i)
+            up = dot(normed, n.wf[0, cols, :], 1, 1)
+            d_act = dot(cot, n.wf[1, cols, :], 1, 1)
+            cdf = 0.5 + 0.5 * lax.erf(up * (0.5**0.5))
+            n.act[s, :, cols] = (up * cdf).astype(BF16)
+            slope = cdf + up * (jnp.exp(-0.5 * up * up) * (2.0 * jnp.pi) ** (-0.5))
+            n.d_up[s, :, cols] = (slope * d_act).astype(BF16)
+            return carry
+
+        lax.fori_loop(0, hidden // tile, body, 0)
+        return dot(n.d_up[s], n.wf[0])
+
+    for r in range(2):
+        middle = n.raw[r].astype(F32) + branch.total(r)
+        n.wide[r] = middle
+        n.normed_ffn[mine(r)] = adapt(normalize(middle)[0], table_ffn)
+        share = k.swap(n.normed_ffn.at[mine(r)], n.normed_ffn.at[mine(r)], k.sib)
+        share.start()
+        share.wait_recv()
+        back.give(r, hidden_part(theirs(r)))
+        back.send_x(r, back.pair_sum(r, hidden_part(mine(r))))
+
+    grid_down = GridReduce(k, n.g_down, n.h_down, n.p_down)
+    grid_up = GridReduce(k, n.g_up, n.h_up, n.p_up)
+
+    def spread(target, rows, made):
+        for d in range(target.shape[0]):
+            target[d, rows, :] = made[:, d * LANES : (d + 1) * LANES].astype(BF16)
+
+    def ffn_grads(target, left, right):
+        def body(i, carry):
+            lhs = left[:, :, span(i)].reshape(seq, tile)
+            spread(target, span(i), dot(lhs, right[...].reshape(seq, width), 0, 0))
+            return carry
+
+        lax.fori_loop(0, hidden // tile, body, 0)
+
+    ffn_grads(n.g_down, n.act, n.cot)
+    grid_down.send_y()
+    ffn_grads(n.g_up, n.d_up, n.normed_ffn)
+    grid_up.send_y()
+
+    def down_part(s):
+        return dot(n.act[s], n.wf[1])
+
+    k.finish()
+    out_sum = Settle(branch, shards, n.x_out.at[0], n.s_in, down_part)
+    n.kept[...] = out_sum.kept
+
+    n.d_keys[...] = jnp.zeros_like(n.d_keys)
+    n.d_values[...] = jnp.zeros_like(n.d_values)
+    table_grad = [jnp.zeros((1, width), F32), jnp.zeros((1, width), F32)]
+
+    def prepare(s):
+        d_attn_t = dot(n.wa[3], n.d_branch[s], 1, 1).astype(BF16)
+        row = lax.broadcasted_iota(jnp.int32, (heads_wide, block), 0) // HD
+        product = d_attn_t.astype(F32) * n.attn_t[s].astype(F32)
+        for h in range(heads):
+            rows = slice(h * HD, (h + 1) * HD)
+            cols = slice(h * block, (h + 1) * block)
+            n.delta[s, :, cols] = jnp.sum(product[rows], axis=0, keepdims=True)
+            n.d_mixed[s, :, cols] = jnp.where(row == h, d_attn_t, 0).astype(BF16)
+
+    def attend_back(s, first, last):
+        q4 = n.q4[s]
+        d_mixed = n.d_mixed[s]
+
+        def body(c, carry):
+            scores = dot(n.keys[c], q4, 1, 1)
+            slot = lax.broadcasted_iota(jnp.int32, scores.shape, 0)
+            limit = jnp.where(c == far, far_len, block)
+            prob = jnp.where(slot < limit, jnp.exp(scores - n.log_total[s]), 0.0)
+            low = prob.astype(BF16)
+            d_prob = dot(n.values[c], d_mixed)
+            d_scores = (prob * (d_prob - n.delta[s])).astype(BF16)
+            n.d_values[c] += dot(low, d_mixed, 1, 1)
+            n.d_keys[c] += dot(d_scores, q4)
+            for h in range(heads):
+                rows = slice(h * HD, (h + 1) * HD)
+                n.d_query[s, rows, :] += dot(
+                    n.keys_t[c, rows, :], d_scores[:, h * block : (h + 1) * block]
+                )
+            return carry
+
+        lax.fori_loop(first, last, body, 0)
+
+    n.d_query[...] = jnp.zeros_like(n.d_query)
+    for r in range(2):
+        d_values, d_gain, d_shift = norm_back(n.wide[r], table_ffn, back.total(r))
+        table_grad[0] = table_grad[0] + d_gain
+        table_grad[1] = table_grad[1] + d_shift
+        d_middle = n.cot[mine(r)].astype(F32) + d_values
+        n.wide[2 + r] = d_middle
+        n.d_branch[mine(r)] = d_middle.astype(BF16)
+        share = k.swap(n.d_branch.at[mine(r)], n.d_branch.at[mine(r)], k.sib)
+        share.start()
+        share.wait_recv()
+
+        def both(i, carry, r=r):
+            prepare(2 * r + i)
+            attend_back(2 * r + i, far, far + 1)
+            return carry
+
+        lax.fori_loop(0, 2, both, 0)
+        if r == 0:
+
+            def rest(i, carry, r=r):
+                attend_back(2 * r + i, 0, mp_size)
+                return carry
+
+            lax.fori_loop(0, 2, rest, 0)
+            grid_down.serve()
+            grid_down.wait_y()
+
+    def table_blocks(target, gain, shift):
+        row = lax.broadcasted_iota(jnp.int32, (n.t_ffn.shape[1], width), 0)
+        both = jnp.where(lax.rem(row, 2) == 0, gain, shift)
+        both = jnp.where(row // 2 == code, both, 0.0)
+        for d in range(target.shape[0]):
+            target[d] = both[:, d * LANES : (d + 1) * LANES]
+
+    far_grad = jnp.concatenate([n.d_keys[far], n.d_values[far]], axis=0)
+    n.y_out2[...] = jnp.where(same_y, 0.0, far_grad).astype(BF16)
+    y_grads = k.swap(n.y_out2, n.y_in2, k.ypeer)
+    y_grads.start()
+    table_blocks(n.t_ffn, table_grad[0], table_grad[1])
+    grid_t_ffn = GridReduce(k, n.t_ffn, n.ht_ffn, n.pt_ffn)
+    grid_t_ffn.send_y()
+    gather.wait_sends()
+    line = LineReduce(k, n.far_held, n.far_passing)
+
+    def rest_last(i, carry):
+        attend_back(2 + i, 0, mp_size)
+        return carry
+
+    lax.fori_loop(0, 1, rest_last, 0)
+    y_grads.wait_recv()
+    back_grad = n.y_in2[...].astype(F32)
+    for d in line.order():
+        here = jnp.where(jnp.logical_and(same_y, part_z == d), far_grad, 0.0)
+        there = jnp.where(jnp.logical_and(other_y == k.y, other_z == d), back_grad, 0.0)
+        n.far_held[d] = (here + there).astype(BF16)
+        line.move(d)
+    lax.fori_loop(1, 2, rest_last, 0)
+    grid_up.serve()
+
+    grid_attn = GridReduce(k, n.g_attn, n.h_attn, n.p_attn)
+
+    def add_products(left, right):
+        total = dot(left[0], right[0])
+        for s in range(1, mp_size):
+            total = total + dot(left[s], right[s])
+        return total
+
+    spread(n.g_attn, slice(3 * heads_wide, 4 * heads_wide), add_products(n.attn_t, n.d_branch))
+    for s in range(mp_size):
+        n.d_query_low[s] = (n.d_query[s] * HD ** (-0.5)).astype(BF16)
+    spread(n.g_attn, slice(0, heads_wide), add_products(n.d_query_low, n.normed))
+    grid_t_ffn.serve()
+
+    def take_back(total):
+        n.far_sum[...] = total.astype(BF16)
+
+    line.finish(take_back)
+    from_slot = lax.broadcasted_iota(jnp.int32, (seq, block), 1)
+    to_frame = lax.broadcasted_iota(jnp.int32, (seq, block), 0)
+    unwindow = (to_frame == from_slot + start).astype(F32).astype(BF16)
+    for ref, low, rows in (
+        (n.d_keys, n.d_keys_low, slice(0, block)),
+        (n.d_values, n.d_values_low, slice(block, 2 * block)),
+    ):
+        own = ref[0:mp_size].reshape(seq, heads_wide)
+        total = own + dot(unwindow, n.far_sum[rows, :])
+        low[0:mp_size] = total.astype(BF16).reshape(mp_size, block, heads_wide)
+
+    flat_normed = n.normed[...].reshape(seq, width)
+    for w, low in ((1, n.d_keys_low), (2, n.d_values_low)):
+        made = dot(low[0:mp_size].reshape(seq, heads_wide), flat_normed, 0, 0)
+        spread(n.g_attn, slice(w * heads_wide, (w + 1) * heads_wide), made)
+    grid_attn.send_y()
+
+    def input_part(s):
+        return (
+            dot(n.d_query_low[s], n.wa[0], 0, 0)
+            + dot(n.d_keys_low[s], n.wa[1])
+            + dot(n.d_values_low[s], n.wa[2])
+        )
+
+    k.finish()
+    n.output[...] = (n.wide[k.x] + out_sum.total(n.kept[...])).astype(BF16)
+    in_sum = Settle(back, shards, n.x_out2.at[0], n.x_in.at[0], input_part)
+    n.kept[...] = in_sum.kept
+
+    quarter = heads_wide
+
+    def store_ffn(s):
+        def store(total):
+            n.grad_ffn[pl.ds(s, hidden, stride=2), :] = total
+
+        return store
+
+    def store_attn(total):
+        for s in range(4):
+            n.grad_attn[pl.ds(s, quarter, stride=4), :] = total[s * quarter : (s + 1) * quarter]
+
+    d_values, d_gain, d_shift = norm_back(n.raw[k.x].astype(F32), table_attn, in_sum.total(n.kept[...]))
+    n.grad_tokens[...] = (n.wide[2 + k.x] + d_values).astype(BF16)
+    table_blocks(n.t_attn, d_gain, d_shift)
+    grid_t_attn = GridReduce(k, n.t_attn, n.ht_attn, n.pt_attn)
+    grid_t_attn.send_y()
+    grid_attn.serve()
+    grid_t_attn.serve()
+    grid_down.finish(store_ffn(1))
+    grid_up.finish(store_ffn(0))
+
+    def store_table(over_x):
+        def store(total):
+            n.t_out[over_x, 0] = total
+            pair = k.swap(n.t_out.at[over_x, 0], n.t_in.at[over_x, 0], k.sib)
+            pair.start()
+            pair.wait_recv()
+            total = total + n.t_in[over_x, 0]
+            if over_x:
+                n.t_out[over_x, 1] = total
+                along = k.swap(n.t_out.at[over_x, 1], n.t_in.at[over_x, 1], k.xpeer)
+                along.start()
+                along.wait_recv()
+                total = total + n.t_in[over_x, 1]
+            piece = LANES // mp_size
+            kept = total
+            for m in range(1, mp_size):
+                turned = pltpu.roll(total, LANES - m * piece, 1)
+                kept = jnp.where(k.mp == m, turned, kept)
+            n.grad_ada[over_x] = kept
+
+        return store
+
+    grid_t_ffn.finish(store_table(0))
+    grid_t_attn.finish(store_table(1))
+    grid_attn.finish(store_attn)
+    k.finish()
+    line.wait_sends()
+    for unit in (grid_down, grid_up, grid_attn, grid_t_ffn, grid_t_attn):
+        unit.wait_sends()
+        if unit is not grid_down:
+            unit.wait_y()
+
+
+def layer(tokens, cotangent, w_attn, w_ffn, ada_attn, ada_ffn, ints, dp_size, mp_size):
+    z_size = dp_size // 2
+    block, width = tokens.shape
+    heads_wide = w_attn.shape[1]
+    hidden = w_ffn.shape[1]
+    heads = heads_wide // HD
+    table_rows = ada_attn.shape[0] * 2
+    lane_block = width // dp_size
+
+    inputs = dict(
+        tokens=tokens,
+        cotangent=cotangent,
+        w_attn=w_attn,
+        w_ffn=w_ffn,
+        ada_attn=ada_attn,
+        ada_ffn=ada_ffn,
+        **ints,
+    )
+    spaces = dict.fromkeys(("tokens", "cotangent", "w_attn", "w_ffn"), pl.ANY)
+    spaces.update(dict.fromkeys(ints, pltpu.SMEM))
+    outputs = dict(
+        output=((block, width), BF16),
+        grad_tokens=((block, width), BF16),
+        grad_attn=((4 * heads_wide, lane_block), F32),
+        grad_ffn=((2 * hidden, lane_block), F32),
+        grad_ada=((2, table_rows, lane_block), F32),
+    )
+    wide = (mp_size, block, width)
+    two = (2, block, width)
+    square = (mp_size + 1, block, heads_wide)
+    attn_rows, window = 4 * heads_wide, 2 * block
+    low, full = {}, {}
+    for name in ("normed", "cot", "normed_ffn", "act", "d_up"):
+        low[name] = wide
+    low.update(raw=two, wa=w_attn.shape, wf=w_ffn.shape)
+    for name in ("keys", "values", "keys_t", "values_t"):
+        low[name] = square
+    low.update(q4=(mp_size, heads * block, heads_wide), attn_t=(mp_size, heads_wide, block))
+    for name in ("pair_out", "pair_in", "x_out", "x_in", "x_out2", "x_in2"):
+        low[name] = two
+    low.update(s_in=(block, width), windows=(z_size, window, heads_wide))
+    low.update(far_passing=(z_size + 1, window, heads_wide), far_sum=(window, heads_wide))
+    for name in ("y_out", "y_in", "y_out2", "y_in2"):
+        low[name] = (window, heads_wide)
+    for name, rows in (("up", hidden), ("down", hidden), ("attn", attn_rows)):
+        if name != "attn":
+            low["g_" + name] = (dp_size, rows, lane_block)
+        low["h_" + name] = (z_size, rows, lane_block)
+        low["p_" + name] = (z_size + 1, rows, lane_block)
+    for name in ("_ffn", "_attn"):
+        full["t" + name] = (dp_size, table_rows, lane_block)
+        full["ht" + name] = (z_size, table_rows, lane_block)
+        full["pt" + name] = (z_size + 1, table_rows, lane_block)
+    full.update(t_out=(2, 2, table_rows, lane_block), t_in=(2, 2, table_rows, lane_block))
+    full.update(wide=(mp_size, block, heads * block), kept=(block, width))
+    for name in ("top", "total", "log_total", "delta"):
+        full[name] = (mp_size, 1, heads * block)
+    full.update(mixed=(mp_size, heads_wide, block))
+    full.update(d_keys=square, d_values=square)
+    scratch = {name: pltpu.VMEM(shape, BF16) for name, shape in low.items()}
+    scratch.update({name: pltpu.VMEM(shape, F32) for name, shape in full.items()})
+    copies = 160
+    scratch.update(
+        load_sem=pltpu.SemaphoreType.DMA((4,)),
+        send_sem=pltpu.SemaphoreType.DMA((copies,)),
+        recv_sem=pltpu.SemaphoreType.DMA((copies,)),
+    )
+    names = tuple(inputs) + tuple(outputs) + tuple(scratch)
+    return pl.pallas_call(
+        functools.partial(layer_kernel, names, z_size),
+        out_shape=tuple(jax.ShapeDtypeStruct(*shape) for shape in outputs.values()),
+        in_specs=[pl.BlockSpec(memory_space=spaces.get(name, pltpu.VMEM)) for name in inputs],
+        out_specs=[pl.BlockSpec(memory_space=pltpu.VMEM) for _ in outputs],
+        scratch_shapes=list(scratch.values()),
+        compiler_params=pltpu.CompilerParams(
+            collective_id=1, has_side_effects=True, vmem_limit_bytes=60 << 20
+        ),
+    )(*inputs.values())
 
 
 def shards(
@@ -110,6 +950,38 @@
     head_cols = w_attn.shape[0]
     heads_here = head_cols // HD
     total_rows = codebook.shape[0]
+    dp_size = lax.axis_size("dp")
+    fits = width == dp_size * LANES and width == w_ffn.shape[0] == tok_rows * heads_here
+    if seq_here == 1 and mp_size == 4 and fits and tok_rows == PMAX:
+        ints = dict(
+            codebook=codebook,
+            group_sizes=group_sizes,
+            partner_pick=partner_pick,
+            prompt_start=prompt_start,
+            prompt_len=prompt_len,
+        )
+        results = layer(
+            tokens,
+            cotangent,
+            jnp.swapaxes(w_attn, 0, 1),
+            jnp.swapaxes(w_ffn, 0, 1),
+            ada_attn,
+            ada_ffn,
+            ints,
+            dp_size,
+            mp_size,
+        )
+        output, grad_tokens, grad_attn, grad_ffn, grad_ada = results
+        grad_ada = grad_ada[:, :, : width // (dp_size * mp_size)]
+        grad_ada = grad_ada.reshape((2,) + ada_attn.shape[:2] + grad_ada.shape[2:])
+        return (
+            output,
+            grad_tokens,
+            grad_attn.reshape(head_cols, 4, LANES),
+            grad_ffn.reshape(w_ffn.shape[0], 2, LANES),
+            grad_ada[1],
+            grad_ada[0],
+        )
     partner = partner_rows(group_sizes, partner_pick)
     first_row = dp_index * seq_here
     tok_global = (dp_index * mp_size + mp_index) * tok_rows + jnp.arange(tok_rows, dtype=jnp.int32)

time: 904 us -> 272 us (0.30)
  waiting for transfers between devices: 625 us -> 0 us
  Pallas kernels: 0 us -> 252 us
  matrix products: 121 us -> 0 us
  local copies, waits for them, and re-layouts: 76 us -> 16.1 us
  other arithmetic: 58.2 us -> 0 us
  between operations: 16.9 us -> 1.09 us
    unnamed x17 -> x0, waiting for transfers between devices: 336 us -> none
    pallas_call x0 -> x1, Pallas kernels: none -> 252 us  [layer(): pl.pallas_call(functools.partial(layer_kernel, names, z_size), out_shape=...]
    reduce_scatter x6 -> x0, waiting for transfers between devices: 183 us -> none  [the longest x1 54.6 us: shards(): lax.psum_scatter(grad_attn_local.astype(jnp.bfloat16), 'dp', scatter_dime...]
    dot_general x23 -> x0, matrix products: 121 us -> none  [the longest x3 27.7 us: inner_cols(): lax.dot_general(left, right, (((1,), (1,)), ((), ())), preferred_element_...]
    all_gather x5 -> x0, waiting for transfers between devices: 107 us -> none  [the longest x1 42.1 us: shards(): shard_rows = lax.all_gather(windows, 'dp', axis=0, tiled=True)]
    unnamed x101 -> x8, local copies, waits for them, and re-layouts: 45.2 us -> 14.8 us
    convert_element_type x6 -> x0, other arithmetic: 22.5 us -> none  [the longest x1 14.2 us: attend_back(): d_scores = (attn_prob * (d_prob - row_delta)).astype(jnp.bfloat16)]
    reduce_sum x13 -> x0, other arithmetic: 19.5 us -> none  [the longest x4 7.96 us: adaptive_norm(): center = inputs - jnp.mean(inputs, axis=-1, keepdims=True)]
  transfers between devices with their start and end apart: 14 -> 0, of which waited for: 14 -> 0; matrix products, arithmetic and copies ran while one was open for 16% -> 0% of each run, Pallas kernels for 0% -> 0%
where the time goes in v2:
time: 272 us; the launch traced here: 270 us
  Pallas kernels  252 us (93%)
  local copies, waits for them, and re-layouts  16.1 us (6%)
    pallas_call x1, Pallas kernels, layer(): pl.pallas_call(functools.partial(layer_kernel, names, z_size), out_shape=...  252 us
    unnamed x8, local copies, waits for them, and re-layouts  14.8 us

profile of v2, /device:TPU:0, one launch (start us, length us, event | category | flops | bytes accessed | tf_op | source)
XLA Modules:
  0.0 269.6 jit_solution(4425957935077832889)
XLA Ops:
  0.6 0.0 copy-start
  0.6 3.7 %copy.22 = bf16[256,4,1024]{2,0,1:T(8,128)(2,1)} copy(bf16[256,4,1024]{2,1,0:T(4,128)(2,1)} %param.12) | data formatting | bytes 4194304 | tf_op args[1]
  4.3 0.0 copy-done
  4.3 3.2 %copy.21 = bf16[1024,2,1024]{2,0,1:T(8,128)(2,1)} copy(bf16[1024,2,1024]{2,1,0:T(2,128)(2,1)S(1)} %copy-done) | data formatting | bytes 8388608 | tf_op args[2]
  7.6 252.4 %shard_map.154 = (bf16[256,1024]{1,0:T(8,128)(2,1)}, bf16[256,1024]{1,0:T(8,128)(2,1)}, f32[1024,128]{1,0:T(8,128)}, f32[2048,128]{1,0:T(8,128)}, f32[2,16,128]{2,1,0:T(8,128)}) custom-call(bf16[256,1024]{1,0:T(8,128)(2,1)} %refs_0_.1, bf16[256,1024]{1,0:T(8,128)(2,1)} %refs_1_.1, bf16[4,256,1024]{2,1,0:T(8,128)(2,1)} %bitcast.11, ...), custom_call_target="tpu_custom_call" | custom-call | tf_op jit(solution)/shard_map/pallas_call | solution.py:919
  260.0 1.3 fusion
  261.3 1.9 copy.27
  263.2 1.9 copy.28
  265.0 1.9 copy.29
  266.9 2.3 copy.30
Async XLA Ops:
  0.6 3.7 %copy-start = (bf16[1024,2,1024]{2,1,0:T(2,128)(2,1)S(1)}, bf16[1024,2,1024]{2,1,0:T(2,128)(2,1)}, u32[]{:S(2)}) copy-start(bf16[1024,2,1024]{2,1,0:T(2,128)(2,1)} %param.13) | copy-start | bytes 12582916

commit v3 on v2

--- a/solution.py
+++ b/solution.py
@@ -110,6 +110,7 @@
         self.dp = lax.axis_index("dp")
         self.mp = lax.axis_index("mp")
         self.z_size = z_size
+        self.order = (z_size - 1, 0) + tuple(range(1, z_size - 1))
         self.y = lax.rem(self.dp, 2)
         self.z = self.dp // 2
         self.core = lax.rem(self.mp, 2)
@@ -178,10 +179,6 @@
         self.nr = links.take(links.z_size)
         self.nl = links.take(links.z_size)
 
-    def order(self):
-        n = self.k.z_size
-        return [n - 1, 0] + list(range(1, n - 1))
-
     def z_copy(self, d, rightward):
         k = self.k
         if rightward:
@@ -193,26 +190,38 @@
         total = self.held[d].astype(F32) + self.passing[d].astype(F32)
         self.held[d] = total.astype(self.held.dtype)
 
-    def move(self, d):
+    def begin(self, d):
         k = self.k
-
-        @pl.when(k.z < d)
+        last = k.z_size - 1
+        if d > 0:
+
+            @pl.when(k.z == 0)
+            def _():
+                self.z_copy(d, True).start()
+
+        if d < last:
+
+            @pl.when(k.z == last)
+            def _():
+                self.z_copy(d, False).start()
+
+    def step(self, i):
+        k = self.k
+        n = k.z_size
+
+        @pl.when(k.z == i)
         def _():
-            @pl.when(k.z > 0)
-            def _():
+            for d in range(n - 1, i, -1):
                 self.z_copy(d, True).wait_recv()
                 self.add(d)
-
-            self.z_copy(d, True).start()
-
-        @pl.when(k.z > d)
+                self.z_copy(d, True).start()
+
+        @pl.when(k.z == n - 1 - i)
         def _():
-            @pl.when(k.z < k.z_size - 1)
-            def _():
+            for d in range(n - 1 - i):
                 self.z_copy(d, False).wait_recv()
                 self.add(d)
-
-            self.z_copy(d, False).start()
+                self.z_copy(d, False).start()
 
     def finish(self, store):
         k = self.k
@@ -255,19 +264,22 @@
         other = 2 * d + 1 - k.y
         return k.copy(self.local.at[other], self.held.at[d], self.ny + d, k.ypeer)
 
-    def send_y(self):
-        for d in self.order():
-            self.y_copy(d).start()
+    def send_y(self, d):
+        self.y_copy(d).start()
+
+    def send_all(self):
+        for d in self.k.order:
+            self.send_y(d)
 
     def merge_y(self, d):
         self.y_copy(d).wait_recv()
         total = self.local[2 * d + self.k.y].astype(F32) + self.held[d].astype(F32)
         self.held[d] = total.astype(self.held.dtype)
 
-    def serve(self):
-        for d in self.order():
+    def take(self, *dests):
+        for d in dests:
             self.merge_y(d)
-            self.move(d)
+            self.begin(d)
 
     def wait_y(self):
         for d in range(self.k.z_size):
@@ -403,7 +415,6 @@
         d_mixed=held["act"],
         d_query=held["mixed"],
         d_branch=held["normed_ffn"],
-        far_held=held["windows"],
         d_query_low=held["attn_t"],
         d_keys_low=held["keys_t"],
         d_values_low=held["values_t"],
@@ -517,10 +528,11 @@
     from_row = lax.broadcasted_iota(jnp.int32, (block, seq), 1)
     to_row = lax.broadcasted_iota(jnp.int32, (block, seq), 0)
     window = (from_row == to_row + start).astype(F32).astype(BF16)
-    n.windows[k.z, 0:block] = dot(window, all_keys).astype(BF16)
-    n.windows[k.z, block : 2 * block] = dot(window, all_values).astype(BF16)
-    gather = LineGather(k, n.windows)
-    gather.start()
+    gathers = []
+    for half, source in ((n.windows_k, all_keys), (n.windows_v, all_values)):
+        half[k.z] = dot(window, source).astype(BF16)
+        gathers.append(LineGather(k, half))
+        gathers[-1].start()
 
     def attend_own(s, carry):
         q4 = n.q4[s]
@@ -542,27 +554,27 @@
         n.total[s] = total
         return carry
 
+    y_windows = []
     for s in range(mp_size):
-        attend_own_s = functools.partial(attend_own)
-        lax.fori_loop(s, s + 1, attend_own_s, 0)
+        lax.fori_loop(s, s + 1, attend_own, 0)
         if 0 < s < z_size:
-            gather.serve(s)
-    for distance in range(mp_size, z_size):
-        gather.serve(distance)
-
-    n.y_out[...] = n.windows[other_z]
-    y_window = k.swap(n.y_out, n.y_in, k.ypeer)
-    y_window.start()
+            for half in range(2):
+                gathers[half].serve(s)
+                if s == z_size - 1:
+                    n.y_out[half] = gathers[half].slots[other_z]
+                    y_windows.append(k.swap(n.y_out.at[half], n.y_in.at[half], k.ypeer))
+                    y_windows[-1].start()
+
     cot_x.wait_recv()
     cot_pass = k.swap(n.cot.at[x_shard], n.cot.at[x_shard], k.sib)
     cot_pass.start()
-    y_window.wait_recv()
     same_y = part_y == k.y
-    far_kv = jnp.where(same_y, n.windows[part_z].astype(F32), n.y_in[...].astype(F32))
-    n.keys[far] = far_kv[0:block].astype(BF16)
-    n.values[far] = far_kv[block:].astype(BF16)
-    n.keys_t[far] = far_kv[0:block].T.astype(BF16)
-    n.values_t[far] = far_kv[block:].T.astype(BF16)
+    for half, (ref, turned) in enumerate(((n.keys, n.keys_t), (n.values, n.values_t))):
+        y_windows[half].wait_recv()
+        here = gathers[half].slots[part_z].astype(F32)
+        far_rows = jnp.where(same_y, here, n.y_in[half].astype(F32))
+        ref[far] = far_rows.astype(BF16)
+        turned[far] = far_rows.T.astype(BF16)
 
     def attend_far(s):
         scores = dot(n.keys[far], n.q4[s], 1, 1)
@@ -612,12 +624,14 @@
         lax.fori_loop(0, hidden // tile, body, 0)
         return dot(n.d_up[s], n.wf[0])
 
+    shares = []
     for r in range(2):
         middle = n.raw[r].astype(F32) + branch.total(r)
         n.wide[r] = middle
         n.normed_ffn[mine(r)] = adapt(normalize(middle)[0], table_ffn)
         share = k.swap(n.normed_ffn.at[mine(r)], n.normed_ffn.at[mine(r)], k.sib)
         share.start()
+        shares.append(share)
         share.wait_recv()
         back.give(r, hidden_part(theirs(r)))
         back.send_x(r, back.pair_sum(r, hidden_part(mine(r))))
@@ -638,14 +652,13 @@
         lax.fori_loop(0, hidden // tile, body, 0)
 
     ffn_grads(n.g_down, n.act, n.cot)
-    grid_down.send_y()
+    grid_down.send_all()
     ffn_grads(n.g_up, n.d_up, n.normed_ffn)
-    grid_up.send_y()
 
     def down_part(s):
         return dot(n.act[s], n.wf[1])
 
-    k.finish()
+    k.finish(branch.along_x[0])
     out_sum = Settle(branch, shards, n.x_out.at[0], n.s_in, down_part)
     n.kept[...] = out_sum.kept
 
@@ -693,6 +706,7 @@
         table_grad[1] = table_grad[1] + d_shift
         d_middle = n.cot[mine(r)].astype(F32) + d_values
         n.wide[2 + r] = d_middle
+        k.finish(shares[r])
         n.d_branch[mine(r)] = d_middle.astype(BF16)
         share = k.swap(n.d_branch.at[mine(r)], n.d_branch.at[mine(r)], k.sib)
         share.start()
@@ -710,9 +724,10 @@
                 attend_back(2 * r + i, 0, mp_size)
                 return carry
 
-            lax.fori_loop(0, 2, rest, 0)
-            grid_down.serve()
-            grid_down.wait_y()
+            lax.fori_loop(0, 1, rest, 0)
+            grid_down.take(k.order[0])
+            lax.fori_loop(1, 2, rest, 0)
+            grid_down.take(k.order[1])
 
     def table_blocks(target, gain, shift):
         row = lax.broadcasted_iota(jnp.int32, (n.t_ffn.shape[1], width), 0)
@@ -721,32 +736,45 @@
         for d in range(target.shape[0]):
             target[d] = both[:, d * LANES : (d + 1) * LANES]
 
-    far_grad = jnp.concatenate([n.d_keys[far], n.d_values[far]], axis=0)
-    n.y_out2[...] = jnp.where(same_y, 0.0, far_grad).astype(BF16)
-    y_grads = k.swap(n.y_out2, n.y_in2, k.ypeer)
-    y_grads.start()
+    y_grads = []
+    for half, ref in enumerate((n.d_keys, n.d_values)):
+        k.finish(y_windows[half])
+        n.y_out[half] = jnp.where(same_y, 0.0, ref[far]).astype(BF16)
+        y_grads.append(k.swap(n.y_out.at[half], n.y_in.at[half], k.ypeer))
+        y_grads[half].start()
     table_blocks(n.t_ffn, table_grad[0], table_grad[1])
     grid_t_ffn = GridReduce(k, n.t_ffn, n.ht_ffn, n.pt_ffn)
-    grid_t_ffn.send_y()
-    gather.wait_sends()
-    line = LineReduce(k, n.far_held, n.far_passing)
+    grid_t_ffn.send_all()
+    grid_up.send_all()
+    lines = []
+    for gather, held, passing in (
+        (gathers[0], n.windows_k, n.passing_k),
+        (gathers[1], n.windows_v, n.passing_v),
+    ):
+        gather.wait_sends()
+        lines.append(LineReduce(k, held, passing))
 
     def rest_last(i, carry):
         attend_back(2 + i, 0, mp_size)
         return carry
 
     lax.fori_loop(0, 1, rest_last, 0)
-    y_grads.wait_recv()
-    back_grad = n.y_in2[...].astype(F32)
-    for d in line.order():
-        here = jnp.where(jnp.logical_and(same_y, part_z == d), far_grad, 0.0)
-        there = jnp.where(jnp.logical_and(other_y == k.y, other_z == d), back_grad, 0.0)
-        n.far_held[d] = (here + there).astype(BF16)
-        line.move(d)
+    for half, ref in enumerate((n.d_keys, n.d_values)):
+        y_grads[half].wait_recv()
+        back_grad = n.y_in[half].astype(F32)
+        for d in k.order:
+            here = jnp.where(jnp.logical_and(same_y, part_z == d), ref[far], 0.0)
+            there = jnp.where(jnp.logical_and(other_y == k.y, other_z == d), back_grad, 0.0)
+            lines[half].held[d] = (here + there).astype(BF16)
+            lines[half].begin(d)
     lax.fori_loop(1, 2, rest_last, 0)
-    grid_up.serve()
-
-    grid_attn = GridReduce(k, n.g_attn, n.h_attn, n.p_attn)
+    for line in lines:
+        line.step(1)
+    grid_down.take(*k.order[2:])
+    grid_down.wait_y()
+
+    grid_oq = GridReduce(k, n.g_attn.at[:, 0 : 2 * heads_wide], n.h_oq, n.p_oq)
+    grid_kv = GridReduce(k, n.g_attn.at[:, 2 * heads_wide : 4 * heads_wide], n.h_kv, n.p_kv)
 
     def add_products(left, right):
         total = dot(left[0], right[0])
@@ -754,32 +782,37 @@
             total = total + dot(left[s], right[s])
         return total
 
-    spread(n.g_attn, slice(3 * heads_wide, 4 * heads_wide), add_products(n.attn_t, n.d_branch))
+    spread(n.g_attn, slice(0, heads_wide), add_products(n.attn_t, n.d_branch))
+    for line in lines:
+        line.step(2)
     for s in range(mp_size):
         n.d_query_low[s] = (n.d_query[s] * HD ** (-0.5)).astype(BF16)
-    spread(n.g_attn, slice(0, heads_wide), add_products(n.d_query_low, n.normed))
-    grid_t_ffn.serve()
-
-    def take_back(total):
-        n.far_sum[...] = total.astype(BF16)
-
-    line.finish(take_back)
+    spread(n.g_attn, slice(heads_wide, 2 * heads_wide), add_products(n.d_query_low, n.normed))
+    grid_oq.send_all()
+    grid_t_ffn.take(*k.order)
+    grid_down.step(1)
+
+    def take_back(half):
+        def store(total):
+            n.far_sum[half] = total.astype(BF16)
+
+        return store
+
+    for half in range(2):
+        lines[half].finish(take_back(half))
     from_slot = lax.broadcasted_iota(jnp.int32, (seq, block), 1)
     to_frame = lax.broadcasted_iota(jnp.int32, (seq, block), 0)
     unwindow = (to_frame == from_slot + start).astype(F32).astype(BF16)
-    for ref, low, rows in (
-        (n.d_keys, n.d_keys_low, slice(0, block)),
-        (n.d_values, n.d_values_low, slice(block, 2 * block)),
-    ):
+    for half, (ref, low) in enumerate(((n.d_keys, n.d_keys_low), (n.d_values, n.d_values_low))):
         own = ref[0:mp_size].reshape(seq, heads_wide)
-        total = own + dot(unwindow, n.far_sum[rows, :])
+        total = own + dot(unwindow, n.far_sum[half])
         low[0:mp_size] = total.astype(BF16).reshape(mp_size, block, heads_wide)
 
     flat_normed = n.normed[...].reshape(seq, width)
-    for w, low in ((1, n.d_keys_low), (2, n.d_values_low)):
+    for w, low in ((2, n.d_keys_low), (3, n.d_values_low)):
         made = dot(low[0:mp_size].reshape(seq, heads_wide), flat_normed, 0, 0)
         spread(n.g_attn, slice(w * heads_wide, (w + 1) * heads_wide), made)
-    grid_attn.send_y()
+    grid_kv.send_all()
 
     def input_part(s):
         return (
@@ -788,10 +821,14 @@
             + dot(n.d_values_low[s], n.wa[2])
         )
 
-    k.finish()
+    k.finish(back.along_x[0])
     n.output[...] = (n.wide[k.x] + out_sum.total(n.kept[...])).astype(BF16)
     in_sum = Settle(back, shards, n.x_out2.at[0], n.x_in.at[0], input_part)
     n.kept[...] = in_sum.kept
+    grid_t_ffn.step(1)
+    grid_down.step(2)
+    grid_up.take(*k.order)
+    grid_t_ffn.step(2)
 
     quarter = heads_wide
 
@@ -801,18 +838,29 @@
 
         return store
 
-    def store_attn(total):
-        for s in range(4):
-            n.grad_attn[pl.ds(s, quarter, stride=4), :] = total[s * quarter : (s + 1) * quarter]
+    def store_attn(*places):
+        def store(total):
+            for i, s in enumerate(places):
+                rows = total[i * quarter : (i + 1) * quarter]
+                n.grad_attn[pl.ds(s, quarter, stride=4), :] = rows
+
+        return store
 
     d_values, d_gain, d_shift = norm_back(n.raw[k.x].astype(F32), table_attn, in_sum.total(n.kept[...]))
     n.grad_tokens[...] = (n.wide[2 + k.x] + d_values).astype(BF16)
     table_blocks(n.t_attn, d_gain, d_shift)
     grid_t_attn = GridReduce(k, n.t_attn, n.ht_attn, n.pt_attn)
-    grid_t_attn.send_y()
-    grid_attn.serve()
-    grid_t_attn.serve()
+    grid_t_attn.send_all()
     grid_down.finish(store_ffn(1))
+    grid_oq.take(*k.order)
+    grid_up.step(1)
+    grid_t_attn.take(*k.order)
+    grid_oq.step(1)
+    grid_up.step(2)
+    grid_t_attn.step(1)
+    grid_kv.take(*k.order)
+    grid_oq.step(2)
+    grid_t_attn.step(2)
     grid_up.finish(store_ffn(0))
 
     def store_table(over_x):
@@ -838,11 +886,15 @@
         return store
 
     grid_t_ffn.finish(store_table(0))
+    grid_kv.step(1)
     grid_t_attn.finish(store_table(1))
-    grid_attn.finish(store_attn)
+    grid_oq.finish(store_attn(3, 0))
+    grid_kv.step(2)
+    grid_kv.finish(store_attn(1, 2))
     k.finish()
-    line.wait_sends()
-    for unit in (grid_down, grid_up, grid_attn, grid_t_ffn, grid_t_attn):
+    for line in lines:
+        line.wait_sends()
+    for unit in (grid_down, grid_up, grid_oq, grid_kv, grid_t_ffn, grid_t_attn):
         unit.wait_sends()
         if unit is not grid_down:
             unit.wait_y()
@@ -878,7 +930,6 @@
     wide = (mp_size, block, width)
     two = (2, block, width)
     square = (mp_size + 1, block, heads_wide)
-    attn_rows, window = 4 * heads_wide, 2 * block
     low, full = {}, {}
     for name in ("normed", "cot", "normed_ffn", "act", "d_up"):
         low[name] = wide
@@ -888,13 +939,16 @@
     low.update(q4=(mp_size, heads * block, heads_wide), attn_t=(mp_size, heads_wide, block))
     for name in ("pair_out", "pair_in", "x_out", "x_in", "x_out2", "x_in2"):
         low[name] = two
-    low.update(s_in=(block, width), windows=(z_size, window, heads_wide))
-    low.update(far_passing=(z_size + 1, window, heads_wide), far_sum=(window, heads_wide))
-    for name in ("y_out", "y_in", "y_out2", "y_in2"):
-        low[name] = (window, heads_wide)
-    for name, rows in (("up", hidden), ("down", hidden), ("attn", attn_rows)):
-        if name != "attn":
-            low["g_" + name] = (dp_size, rows, lane_block)
+    low.update(s_in=(block, width))
+    for name in ("far_sum", "y_out", "y_in"):
+        low[name] = (2, block, heads_wide)
+    for name in ("k", "v"):
+        low["windows_" + name] = (z_size, block, heads_wide)
+        low["passing_" + name] = (z_size + 1, block, heads_wide)
+    for name in ("up", "down"):
+        low["g_" + name] = (dp_size, hidden, lane_block)
+    half = 2 * heads_wide
+    for name, rows in (("up", hidden), ("down", hidden), ("oq", half), ("kv", half)):
         low["h_" + name] = (z_size, rows, lane_block)
         low["p_" + name] = (z_size + 1, rows, lane_block)
     for name in ("_ffn", "_attn"):
@@ -909,7 +963,7 @@
     full.update(d_keys=square, d_values=square)
     scratch = {name: pltpu.VMEM(shape, BF16) for name, shape in low.items()}
     scratch.update({name: pltpu.VMEM(shape, F32) for name, shape in full.items()})
-    copies = 160
+    copies = 200
     scratch.update(
         load_sem=pltpu.SemaphoreType.DMA((4,)),
         send_sem=pltpu.SemaphoreType.DMA((copies,)),
@@ -926,6 +980,25 @@
             collective_id=1, has_side_effects=True, vmem_limit_bytes=60 << 20
         ),
     )(*inputs.values())
+
+
+def place_kernel(count, *refs):
+    moves = []
+    for i in range(count):
+        moves.append(pltpu.make_async_copy(refs[i], refs[count + i], refs[-1].at[i]))
+        moves[i].start()
+    for move in moves:
+        move.wait()
+
+
+def place(arrays):
+    return pl.pallas_call(
+        functools.partial(place_kernel, len(arrays)),
+        out_shape=tuple(jax.ShapeDtypeStruct(a.shape, a.dtype) for a in arrays),
+        in_specs=[pl.BlockSpec(memory_space=pltpu.VMEM)] * len(arrays),
+        out_specs=[pl.BlockSpec(memory_space=pl.ANY)] * len(arrays),
+        scratch_shapes=[pltpu.SemaphoreType.DMA((len(arrays),))],
+    )(*arrays)
 
 
 def shards(
@@ -971,7 +1044,8 @@
             dp_size,
             mp_size,
         )
-        output, grad_tokens, grad_attn, grad_ffn, grad_ada = results
+        output, grad_tokens, grad_attn, grad_ffn = place(results[:4])
+        grad_ada = results[4]
         grad_ada = grad_ada[:, :, : width // (dp_size * mp_size)]
         grad_ada = grad_ada.reshape((2,) + ada_attn.shape[:2] + grad_ada.shape[2:])
         return (

time: 272 us -> 215 us (0.79)
  Pallas kernels: 252 us -> 204 us
  local copies, waits for them, and re-layouts: 16.1 us -> 8.26 us
    pallas_call x1, Pallas kernels: 252 us -> 200 us  [layer(): pl.pallas_call(functools.partial(layer_kernel, names, z_size), out_shape=...]
    unnamed x8 -> x4, local copies, waits for them, and re-layouts: 14.8 us -> 6.94 us
    pallas_call x0 -> x1, Pallas kernels: none -> 3.23 us  [place(): pl.pallas_call(functools.partial(place_kernel, len(arrays)), out_shape=tu...]
where the time goes in v3:
time: 215 us; the launch traced here: 213 us
  Pallas kernels  204 us (95%)
  local copies, waits for them, and re-layouts  8.26 us (4%)
    pallas_call x1, Pallas kernels, layer(): pl.pallas_call(functools.partial(layer_kernel, names, z_size), out_shape=...  200 us
    unnamed x4, local copies, waits for them, and re-layouts  6.94 us

profile of v3, /device:TPU:0, one launch (start us, length us, event | category | flops | bytes accessed | tf_op | source)
XLA Modules:
  0.0 212.8 jit_solution(18290136984141992022)
XLA Ops:
  0.6 0.0 copy-start
  0.6 3.7 %copy.22 = bf16[256,4,1024]{2,0,1:T(8,128)(2,1)} copy(bf16[256,4,1024]{2,1,0:T(4,128)(2,1)} %param.12) | data formatting | bytes 4194304 | tf_op args[1]
  4.3 0.0 copy-done
  4.3 3.3 %copy.21 = bf16[1024,2,1024]{2,0,1:T(8,128)(2,1)} copy(bf16[1024,2,1024]{2,1,0:T(2,128)(2,1)S(1)} %copy-done) | data formatting | bytes 8388608 | tf_op args[2]
  7.6 200.4 %shard_map.154 = (bf16[256,1024]{1,0:T(8,128)(2,1)}, bf16[256,1024]{1,0:T(8,128)(2,1)}, f32[1024,128]{1,0:T(8,128)}, f32[2048,128]{1,0:T(8,128)}, f32[2,16,128]{2,1,0:T(8,128)}) custom-call(bf16[256,1024]{1,0:T(8,128)(2,1)} %refs_0_.1, bf16[256,1024]{1,0:T(8,128)(2,1)} %refs_1_.1, bf16[4,256,1024]{2,1,0:T(8,128)(2,1)} %bitcast.11, ...), custom_call_target="tpu_custom_call" | custom-call | tf_op jit(solution)/shard_map/pallas_call | solution.py:973
  208.0 3.2 %shard_map.155 = (bf16[256,1024]{1,0:T(8,128)(2,1)}, bf16[256,1024]{1,0:T(8,128)(2,1)}, f32[1024,128]{1,0:T(8,128)}, f32[2048,128]{1,0:T(8,128)}) custom-call(bf16[256,1024]{1,0:T(8,128)(2,1)} %get-tuple-element.15.refs_0_, bf16[256,1024]{1,0:T(8,128)(2,1)} %get-tuple-element.16.refs_1_, f32[1024,128]{1,0:T(8,128)} %get-tuple-element.17.refs_2_, ...), custom_call_target="tpu_custom_call" | custom-call | tf_op jit(solution)/shard_map/pallas_call | solution.py:995
  211.3 1.3 fusion
Async XLA Ops:
  0.6 3.7 %copy-start = (bf16[1024,2,1024]{2,1,0:T(2,128)(2,1)S(1)}, bf16[1024,2,1024]{2,1,0:T(2,128)(2,1)}, u32[]{:S(2)}) copy-start(bf16[1024,2,1024]{2,1,0:T(2,128)(2,1)} %param.13) | copy-start | bytes 12582916

commit v4 on v3

--- a/solution.py
+++ b/solution.py
@@ -131,12 +131,12 @@
         self.used += count
         return first
 
-    def copy(self, src, dst, number, device):
+    def copy(self, src, dst, number, device, landing=None):
         return pltpu.make_async_remote_copy(
             src_ref=src,
             dst_ref=dst,
             send_sem=self.send_sem.at[number],
-            recv_sem=self.recv_sem.at[number],
+            recv_sem=self.recv_sem.at[number if landing is None else landing],
             device_id=device,
             device_id_type=MESH,
         )
@@ -183,8 +183,8 @@
         k = self.k
         if rightward:
             return k.copy(self.held.at[d], self.passing.at[d], self.nr + d, k.right)
-        slot = jnp.where(k.z - 1 == d, k.z_size, d)
-        return k.copy(self.held.at[d], self.passing.at[slot], self.nl + d, k.left)
+        landing = jnp.where(k.z - 1 == d, k.z_size, d)
+        return k.copy(self.held.at[d], self.passing.at[landing], self.nl + d, k.left)
 
     def add(self, d):
         total = self.held[d].astype(F32) + self.passing[d].astype(F32)
@@ -253,33 +253,80 @@
                 self.z_copy(d, False).wait_send()
 
 
-class GridReduce(LineReduce):
+class GridReduce:
     def __init__(self, links, local, held, passing):
-        self.setup(links, held, passing)
-        self.local = local
-        self.ny = links.take(links.z_size)
+        n = links.z_size
+        self.k = links
+        self.local, self.held, self.passing = local, held, passing
+        self.ny, self.ns, self.nr = links.take(n), links.take(n), links.take(n)
+        self.inner = {n - 1: 1, 0: n - 2}
 
     def y_copy(self, d):
         k = self.k
         other = 2 * d + 1 - k.y
         return k.copy(self.local.at[other], self.held.at[d], self.ny + d, k.ypeer)
 
-    def send_y(self, d):
-        self.y_copy(d).start()
-
-    def send_all(self):
-        for d in self.k.order:
-            self.send_y(d)
-
-    def merge_y(self, d):
-        self.y_copy(d).wait_recv()
-        total = self.local[2 * d + self.k.y].astype(F32) + self.held[d].astype(F32)
-        self.held[d] = total.astype(self.held.dtype)
+    def send_y(self, *dests):
+        for d in dests or self.k.order:
+            self.y_copy(d).start()
+
+    def z_copy(self, d):
+        k = self.k
+        to = d
+        if d in self.inner:
+            to = jnp.where(k.z == k.z_size - 1 - d, self.inner[d], d)
+        slot = jnp.where(to == d, k.z, to)
+        device = (2 * to + k.y, k.mp)
+        return k.copy(self.held.at[d], self.passing.at[slot], self.ns + d, device, self.nr + slot)
+
+    def landed(self, slot):
+        self.k.copy(self.held.at[0], self.passing.at[slot], self.ns, self.k.ypeer, self.nr + slot).wait_recv()
 
     def take(self, *dests):
-        for d in dests:
-            self.merge_y(d)
-            self.begin(d)
+        k = self.k
+        for d in dests or k.order:
+            self.y_copy(d).wait_recv()
+            total = self.local[2 * d + k.y].astype(F32) + self.held[d].astype(F32)
+            self.held[d] = total.astype(self.held.dtype)
+            ready = k.z != d
+            if d in self.inner:
+                ready = jnp.logical_and(ready, k.z != self.inner[d])
+
+            @pl.when(ready)
+            def _(d=d):
+                self.z_copy(d).start()
+
+    def step(self):
+        for d, at in self.inner.items():
+
+            @pl.when(self.k.z == at)
+            def _(d=d, at=at):
+                self.landed(at)
+                total = self.held[d].astype(F32) + self.passing[at].astype(F32)
+                self.held[d] = total.astype(self.held.dtype)
+                self.z_copy(d).start()
+
+    def finish(self, store):
+        k = self.k
+        n = k.z_size
+        total = self.held[k.z].astype(F32)
+        for source in range(n):
+            apart = jnp.abs(k.z - source)
+            sends = jnp.logical_and(apart != 0, apart != n - 1)
+
+            @pl.when(sends)
+            def _(source=source):
+                self.landed(source)
+
+            total = total + jnp.where(sends, self.passing[source].astype(F32), 0.0)
+        store(total)
+
+    def wait_sends(self):
+        for d in range(self.k.z_size):
+
+            @pl.when(self.k.z != d)
+            def _(d=d):
+                self.z_copy(d).wait_send()
 
     def wait_y(self):
         for d in range(self.k.z_size):
@@ -387,9 +434,9 @@
         exchange.give(3, term(sib), 1)
         self.kept = exchange.pair_sum(3, term(own))
 
-    def total(self, kept):
+    def total(self):
         self.along_x.wait_recv()
-        return kept + self.x_in[...].astype(F32)
+        return self.x_in[...].astype(F32)
 
 
 def normalize(values):
@@ -482,6 +529,10 @@
     partner = partner_of(k.dp)
     other_partner = partner_of(k.dp + 1 - 2 * k.y)
     part_z, part_y = partner // 2, lax.rem(partner, 2)
+    line_partners = []
+    for d in range(z_size):
+        row = partner_of(2 * d + k.y)
+        line_partners.append((row // 2 == k.z, lax.rem(row, 2) == k.y))
     other_z, other_y = other_partner // 2, lax.rem(other_partner, 2)
     far_len = n.prompt_len[partner]
     table_attn = n.ada_attn[code]
@@ -528,11 +579,13 @@
     from_row = lax.broadcasted_iota(jnp.int32, (block, seq), 1)
     to_row = lax.broadcasted_iota(jnp.int32, (block, seq), 0)
     window = (from_row == to_row + start).astype(F32).astype(BF16)
-    gathers = []
-    for half, source in ((n.windows_k, all_keys), (n.windows_v, all_values)):
-        half[k.z] = dot(window, source).astype(BF16)
-        gathers.append(LineGather(k, half))
-        gathers[-1].start()
+    n.windows_k[k.z] = dot(window, all_keys).astype(BF16)
+    gather = LineGather(k, n.windows_k)
+    gather.start()
+    n.y_out[1] = dot(window, all_values).astype(BF16)
+    y_value = k.swap(n.y_out.at[1], n.y_in.at[1], k.ypeer)
+    y_value.start()
+    line_value = LineReduce(k, n.windows_v, n.passing_v)
 
     def attend_own(s, carry):
         q4 = n.q4[s]
@@ -554,27 +607,45 @@
         n.total[s] = total
         return carry
 
-    y_windows = []
-    for s in range(mp_size):
+    def own(s):
         lax.fori_loop(s, s + 1, attend_own, 0)
-        if 0 < s < z_size:
-            for half in range(2):
-                gathers[half].serve(s)
-                if s == z_size - 1:
-                    n.y_out[half] = gathers[half].slots[other_z]
-                    y_windows.append(k.swap(n.y_out.at[half], n.y_in.at[half], k.ypeer))
-                    y_windows[-1].start()
+
+    own(0)
+    y_value.wait_recv()
+    ours, others = n.y_out[1].astype(F32), n.y_in[1].astype(F32)
+    for d in k.order:
+        here, same_row = line_partners[d]
+        chosen = jnp.where(same_row, ours, others)
+        n.windows_v[d] = jnp.where(here, chosen, 0.0).astype(BF16)
+        line_value.begin(d)
+    gather.serve(1)
+    own(1)
+    line_value.step(1)
+    gather.serve(2)
+    own(2)
+    line_value.step(2)
+    gather.serve(3)
+    n.y_out[0] = n.windows_k[other_z]
+    y_key = k.swap(n.y_out.at[0], n.y_in.at[0], k.ypeer)
+    y_key.start()
+    own(3)
 
     cot_x.wait_recv()
     cot_pass = k.swap(n.cot.at[x_shard], n.cot.at[x_shard], k.sib)
     cot_pass.start()
     same_y = part_y == k.y
-    for half, (ref, turned) in enumerate(((n.keys, n.keys_t), (n.values, n.values_t))):
-        y_windows[half].wait_recv()
-        here = gathers[half].slots[part_z].astype(F32)
-        far_rows = jnp.where(same_y, here, n.y_in[half].astype(F32))
-        ref[far] = far_rows.astype(BF16)
-        turned[far] = far_rows.T.astype(BF16)
+
+    def take_far(ref, turned):
+        def store(rows):
+            ref[far] = rows.astype(BF16)
+            turned[far] = rows.T.astype(BF16)
+
+        return store
+
+    line_value.finish(take_far(n.values, n.values_t))
+    y_key.wait_recv()
+    far_keys = jnp.where(same_y, n.windows_k[part_z].astype(F32), n.y_in[0].astype(F32))
+    take_far(n.keys, n.keys_t)(far_keys)
 
     def attend_far(s):
         scores = dot(n.keys[far], n.q4[s], 1, 1)
@@ -652,7 +723,7 @@
         lax.fori_loop(0, hidden // tile, body, 0)
 
     ffn_grads(n.g_down, n.act, n.cot)
-    grid_down.send_all()
+    grid_down.send_y(*k.order[:3])
     ffn_grads(n.g_up, n.d_up, n.normed_ffn)
 
     def down_part(s):
@@ -719,15 +790,7 @@
 
         lax.fori_loop(0, 2, both, 0)
         if r == 0:
-
-            def rest(i, carry, r=r):
-                attend_back(2 * r + i, 0, mp_size)
-                return carry
-
-            lax.fori_loop(0, 1, rest, 0)
             grid_down.take(k.order[0])
-            lax.fori_loop(1, 2, rest, 0)
-            grid_down.take(k.order[1])
 
     def table_blocks(target, gain, shift):
         row = lax.broadcasted_iota(jnp.int32, (n.t_ffn.shape[1], width), 0)
@@ -736,45 +799,62 @@
         for d in range(target.shape[0]):
             target[d] = both[:, d * LANES : (d + 1) * LANES]
 
-    y_grads = []
-    for half, ref in enumerate((n.d_keys, n.d_values)):
-        k.finish(y_windows[half])
-        n.y_out[half] = jnp.where(same_y, 0.0, ref[far]).astype(BF16)
-        y_grads.append(k.swap(n.y_out.at[half], n.y_in.at[half], k.ypeer))
-        y_grads[half].start()
+    n.packets[k.z] = n.d_values[far].astype(BF16)
+    packets = LineGather(k, n.packets)
+    packets.start()
+    k.finish(y_key)
+    n.y_out[0] = jnp.where(same_y, 0.0, n.d_keys[far]).astype(BF16)
+    y_key = k.swap(n.y_out.at[0], n.y_in.at[0], k.ypeer)
+    y_key.start()
     table_blocks(n.t_ffn, table_grad[0], table_grad[1])
     grid_t_ffn = GridReduce(k, n.t_ffn, n.ht_ffn, n.pt_ffn)
-    grid_t_ffn.send_all()
-    grid_up.send_all()
-    lines = []
-    for gather, held, passing in (
-        (gathers[0], n.windows_k, n.passing_k),
-        (gathers[1], n.windows_v, n.passing_v),
-    ):
-        gather.wait_sends()
-        lines.append(LineReduce(k, held, passing))
-
-    def rest_last(i, carry):
-        attend_back(2 + i, 0, mp_size)
-        return carry
-
-    lax.fori_loop(0, 1, rest_last, 0)
-    for half, ref in enumerate((n.d_keys, n.d_values)):
-        y_grads[half].wait_recv()
-        back_grad = n.y_in[half].astype(F32)
-        for d in k.order:
-            here = jnp.where(jnp.logical_and(same_y, part_z == d), ref[far], 0.0)
-            there = jnp.where(jnp.logical_and(other_y == k.y, other_z == d), back_grad, 0.0)
-            lines[half].held[d] = (here + there).astype(BF16)
-            lines[half].begin(d)
-    lax.fori_loop(1, 2, rest_last, 0)
-    for line in lines:
-        line.step(1)
-    grid_down.take(*k.order[2:])
+    grid_t_ffn.send_y()
+    grid_down.send_y(k.order[3])
+    gather.wait_sends()
+    line_key = LineReduce(k, n.windows_k, n.passing_k)
+
+    def rest(s):
+        def body(s, carry):
+            attend_back(s, 0, mp_size)
+            return carry
+
+        lax.fori_loop(s, s + 1, body, 0)
+
+    rest(0)
+    packets.serve(1)
+    y_key.wait_recv()
+    back_grad = n.y_in[0].astype(F32)
+    for d in k.order:
+        here = jnp.where(jnp.logical_and(same_y, part_z == d), n.d_keys[far], 0.0)
+        there = jnp.where(jnp.logical_and(other_y == k.y, other_z == d), back_grad, 0.0)
+        n.windows_k[d] = (here + there).astype(BF16)
+        line_key.begin(d)
+    rest(1)
+    packets.serve(2)
+    line_key.step(1)
+    rest(2)
+    packets.serve(3)
+    ours = jnp.zeros((block, heads_wide), F32)
+    others = jnp.zeros((block, heads_wide), F32)
+    for d in range(z_size):
+        here, same_row = line_partners[d]
+        packet = n.packets[d].astype(F32)
+        ours = ours + jnp.where(jnp.logical_and(here, same_row), packet, 0.0)
+        others = others + jnp.where(jnp.logical_and(here, jnp.logical_not(same_row)), packet, 0.0)
+    k.finish(y_value)
+    n.y_out[1] = others.astype(BF16)
+    y_value = k.swap(n.y_out.at[1], n.y_in.at[1], k.ypeer)
+    y_value.start()
+    n.d_values[far] = ours
+    line_key.step(2)
+    grid_up.send_y(*k.order[:2])
+    rest(3)
+    grid_down.take(*k.order[1:])
     grid_down.wait_y()
 
-    grid_oq = GridReduce(k, n.g_attn.at[:, 0 : 2 * heads_wide], n.h_oq, n.p_oq)
-    grid_kv = GridReduce(k, n.g_attn.at[:, 2 * heads_wide : 4 * heads_wide], n.h_kv, n.p_kv)
+    half_rows = 2 * heads_wide
+    grid_oq = GridReduce(k, n.g_attn.at[:, 0:half_rows], n.h_oq, n.p_oq)
+    grid_kv = GridReduce(k, n.g_attn.at[:, half_rows : 2 * half_rows], n.h_kv, n.p_kv)
 
     def add_products(left, right):
         total = dot(left[0], right[0])
@@ -783,36 +863,28 @@
         return total
 
     spread(n.g_attn, slice(0, heads_wide), add_products(n.attn_t, n.d_branch))
-    for line in lines:
-        line.step(2)
     for s in range(mp_size):
         n.d_query_low[s] = (n.d_query[s] * HD ** (-0.5)).astype(BF16)
     spread(n.g_attn, slice(heads_wide, 2 * heads_wide), add_products(n.d_query_low, n.normed))
-    grid_oq.send_all()
-    grid_t_ffn.take(*k.order)
-    grid_down.step(1)
-
-    def take_back(half):
-        def store(total):
-            n.far_sum[half] = total.astype(BF16)
-
-        return store
-
-    for half in range(2):
-        lines[half].finish(take_back(half))
+
+    def take_back(total):
+        n.keys_t[far] = total.astype(BF16)
+
+    line_key.finish(take_back)
+    y_value.wait_recv()
+    n.values_t[far] = (n.d_values[far] + n.y_in[1].astype(F32)).astype(BF16)
     from_slot = lax.broadcasted_iota(jnp.int32, (seq, block), 1)
     to_frame = lax.broadcasted_iota(jnp.int32, (seq, block), 0)
     unwindow = (to_frame == from_slot + start).astype(F32).astype(BF16)
-    for half, (ref, low) in enumerate(((n.d_keys, n.d_keys_low), (n.d_values, n.d_values_low))):
+    for ref, low in ((n.d_keys, n.d_keys_low), (n.d_values, n.d_values_low)):
         own = ref[0:mp_size].reshape(seq, heads_wide)
-        total = own + dot(unwindow, n.far_sum[half])
+        total = own + dot(unwindow, low[far])
         low[0:mp_size] = total.astype(BF16).reshape(mp_size, block, heads_wide)
 
     flat_normed = n.normed[...].reshape(seq, width)
     for w, low in ((2, n.d_keys_low), (3, n.d_values_low)):
         made = dot(low[0:mp_size].reshape(seq, heads_wide), flat_normed, 0, 0)
         spread(n.g_attn, slice(w * heads_wide, (w + 1) * heads_wide), made)
-    grid_kv.send_all()
 
     def input_part(s):
         return (
@@ -822,13 +894,25 @@
         )
 
     k.finish(back.along_x[0])
-    n.output[...] = (n.wide[k.x] + out_sum.total(n.kept[...])).astype(BF16)
+    n.output[...] = (n.wide[k.x] + n.kept[...] + out_sum.total()).astype(BF16)
     in_sum = Settle(back, shards, n.x_out2.at[0], n.x_in.at[0], input_part)
     n.kept[...] = in_sum.kept
-    grid_t_ffn.step(1)
-    grid_down.step(2)
-    grid_up.take(*k.order)
-    grid_t_ffn.step(2)
+
+    table_grad = [jnp.zeros((1, width), F32), jnp.zeros((1, width), F32)]
+    for term, at in ((n.x_out2[0].astype(F32), 1 - k.x), (in_sum.kept, k.x)):
+        normed = normalize(n.raw[at].astype(F32))[0]
+        table_grad[0] = table_grad[0] + jnp.sum(term * normed, axis=0, keepdims=True)
+        table_grad[1] = table_grad[1] + jnp.sum(term, axis=0, keepdims=True)
+    table_blocks(n.t_attn, *table_grad)
+    grid_t_attn = GridReduce(k, n.t_attn, n.ht_attn, n.pt_attn)
+    grid_t_attn.send_y()
+    grid_kv.send_y()
+    grid_up.send_y(*k.order[2:])
+    grid_oq.send_y()
+    grid_t_ffn.take()
+    grid_down.step()
+    grid_t_ffn.step()
+    grid_up.take(*k.order[:2])
 
     quarter = heads_wide
 
@@ -841,27 +925,19 @@
     def store_attn(*places):
         def store(total):
             for i, s in enumerate(places):
+                at = pl.ds(s, quarter, stride=4)
                 rows = total[i * quarter : (i + 1) * quarter]
-                n.grad_attn[pl.ds(s, quarter, stride=4), :] = rows
+                n.grad_attn[at, :] = rows
 
         return store
 
-    d_values, d_gain, d_shift = norm_back(n.raw[k.x].astype(F32), table_attn, in_sum.total(n.kept[...]))
+    d_values, _, _ = norm_back(n.raw[k.x].astype(F32), table_attn, n.kept[...] + in_sum.total())
     n.grad_tokens[...] = (n.wide[2 + k.x] + d_values).astype(BF16)
-    table_blocks(n.t_attn, d_gain, d_shift)
-    grid_t_attn = GridReduce(k, n.t_attn, n.ht_attn, n.pt_attn)
-    grid_t_attn.send_all()
+    grid_t_attn.take()
+    grid_kv.take()
     grid_down.finish(store_ffn(1))
-    grid_oq.take(*k.order)
-    grid_up.step(1)
-    grid_t_attn.take(*k.order)
-    grid_oq.step(1)
-    grid_up.step(2)
-    grid_t_attn.step(1)
-    grid_kv.take(*k.order)
-    grid_oq.step(2)
-    grid_t_attn.step(2)
-    grid_up.finish(store_ffn(0))
+    grid_t_attn.step()
+    grid_kv.step()
 
     def store_table(over_x):
         def store(total):
@@ -886,14 +962,18 @@
         return store
 
     grid_t_ffn.finish(store_table(0))
-    grid_kv.step(1)
+    grid_up.take(*k.order[2:])
+    grid_up.step()
     grid_t_attn.finish(store_table(1))
+    grid_kv.finish(store_attn(1, 2))
+    grid_oq.take()
+    grid_up.finish(store_ffn(0))
+    grid_oq.step()
     grid_oq.finish(store_attn(3, 0))
-    grid_kv.step(2)
-    grid_kv.finish(store_attn(1, 2))
     k.finish()
-    for line in lines:
-        line.wait_sends()
+    packets.wait_sends()
+    for unit in (line_value, line_key):
+        unit.wait_sends()
     for unit in (grid_down, grid_up, grid_oq, grid_kv, grid_t_ffn, grid_t_attn):
         unit.wait_sends()
         if unit is not grid_down:
@@ -940,7 +1020,7 @@
     for name in ("pair_out", "pair_in", "x_out", "x_in", "x_out2", "x_in2"):
         low[name] = two
     low.update(s_in=(block, width))
-    for name in ("far_sum", "y_out", "y_in"):
+    for name in ("y_out", "y_in"):
         low[name] = (2, block, heads_wide)
     for name in ("k", "v"):
         low["windows_" + name] = (z_size, block, heads_wide)
@@ -948,13 +1028,14 @@
     for name in ("up", "down"):
         low["g_" + name] = (dp_size, hidden, lane_block)
     half = 2 * heads_wide
+    low.update(packets=(z_size, block, heads_wide))
     for name, rows in (("up", hidden), ("down", hidden), ("oq", half), ("kv", half)):
         low["h_" + name] = (z_size, rows, lane_block)
-        low["p_" + name] = (z_size + 1, rows, lane_block)
+        low["p_" + name] = (z_size, rows, lane_block)
     for name in ("_ffn", "_attn"):
         full["t" + name] = (dp_size, table_rows, lane_block)
         full["ht" + name] = (z_size, table_rows, lane_block)
-        full["pt" + name] = (z_size + 1, table_rows, lane_block)
+        full["pt" + name] = (z_size, table_rows, lane_block)
     full.update(t_out=(2, 2, table_rows, lane_block), t_in=(2, 2, table_rows, lane_block))
     full.update(wide=(mp_size, block, heads * block), kept=(block, width))
     for name in ("top", "total", "log_total", "delta"):

time: 215 us -> 212 us (0.986)
  the two profiles are of different devices: /device:TPU:0 before, /device:TPU:24 now
where the time goes in v4:
time: 212 us; the launch traced here: 210 us
  Pallas kernels  201 us (95%)
  local copies, waits for them, and re-layouts  8.26 us (4%)
    pallas_call x1, Pallas kernels, layer(): pl.pallas_call(functools.partial(layer_kernel, names, z_size), out_shape=...  198 us
    unnamed x4, local copies, waits for them, and re-layouts  6.94 us

profile of v4, /device:TPU:24, one launch (start us, length us, event | category | flops | bytes accessed | tf_op | source)
XLA Modules:
  0.0 210.3 jit_solution(16173413334635276983)
XLA Ops:
  0.6 0.0 copy-start
  0.6 3.7 %copy.22 = bf16[256,4,1024]{2,0,1:T(8,128)(2,1)} copy(bf16[256,4,1024]{2,1,0:T(4,128)(2,1)} %param.12) | data formatting | bytes 4194304 | tf_op args[1]
  4.3 0.0 copy-done
  4.3 3.3 %copy.21 = bf16[1024,2,1024]{2,0,1:T(8,128)(2,1)} copy(bf16[1024,2,1024]{2,1,0:T(2,128)(2,1)S(1)} %copy-done) | data formatting | bytes 8388608 | tf_op args[2]
  7.6 197.8 %shard_map.154 = (bf16[256,1024]{1,0:T(8,128)(2,1)}, bf16[256,1024]{1,0:T(8,128)(2,1)}, f32[1024,128]{1,0:T(8,128)}, f32[2048,128]{1,0:T(8,128)}, f32[2,16,128]{2,1,0:T(8,128)}) custom-call(bf16[256,1024]{1,0:T(8,128)(2,1)} %refs_0_.1, bf16[256,1024]{1,0:T(8,128)(2,1)} %refs_1_.1, bf16[4,256,1024]{2,1,0:T(8,128)(2,1)} %bitcast.11, ...), custom_call_target="tpu_custom_call" | custom-call | tf_op jit(solution)/shard_map/pallas_call | solution.py:1054
  205.4 3.2 %shard_map.155 = (bf16[256,1024]{1,0:T(8,128)(2,1)}, bf16[256,1024]{1,0:T(8,128)(2,1)}, f32[1024,128]{1,0:T(8,128)}, f32[2048,128]{1,0:T(8,128)}) custom-call(bf16[256,1024]{1,0:T(8,128)(2,1)} %get-tuple-element.15.refs_0_, bf16[256,1024]{1,0:T(8,128)(2,1)} %get-tuple-element.16.refs_1_, f32[1024,128]{1,0:T(8,128)} %get-tuple-element.17.refs_2_, ...), custom_call_target="tpu_custom_call" | custom-call | tf_op jit(solution)/shard_map/pallas_call | solution.py:1076
  208.6 1.3 fusion
Async XLA Ops:
  0.6 3.7 %copy-start = (bf16[1024,2,1024]{2,1,0:T(2,128)(2,1)S(1)}, bf16[1024,2,1024]{2,1,0:T(2,128)(2,1)}, u32[]{:S(2)}) copy-start(bf16[1024,2,1024]{2,1,0:T(2,128)(2,1)} %param.13) | copy-start | bytes 12582916
